TPU v7x, 512 devices: a whole 4x4x16 slice. The times are simulated.
512 devices in a mesh: seg: 16 (over z_lo, core), head: 32 (over z_hi, x, y).
Axes of the slice: x: 4, y: 4, z: 16 (z_hi: 2, z_lo: 8; z = z_hi * 8 + z_lo), core: 2. Of those that a mesh axis runs over, the one named last changes fastest.
Arguments:
- queries: bfloat16 [65536, 4096], P(('seg', 'head')), may hold values from -256 to 256
- latent_keys: bfloat16 [768, 4096], P('seg', 'head'), may hold values from -12 to 12
- latent_values: bfloat16 [768, 4096], P('seg', 'head'), may hold values from -6 to 6
- cotangent: bfloat16 [65536, 4096], P(('seg', 'head')), may hold values from -6 to 6
- gate_logits: float32 [32], P('head'), may hold values from 0.3 to 1.5
- visibility: int32 [512, 16], replicated, may hold values from 0 to 1, as said below
- text_counts: int32 [16], replicated, may hold values from 2048 to 4096, as said below
- latent_counts: int32 [16], replicated, may hold values from 2 to 48, as said below
Outputs:
- mixed_rows: bfloat16 [65536, 4096], P(('seg', 'head'))
- grad_queries: bfloat16 [65536, 4096], P(('seg', 'head'))
- grad_keys: bfloat16 [768, 4096], P('seg', 'head')
- grad_values: bfloat16 [768, 4096], P('seg', 'head')
Inputs may be any that keep to these rules, and one draw needn't show every extreme that they name: `visibility`: in the text block's own segment the entry is 1, for later segments it is 0. `text_counts`: one segment has all 4096 rows valid and one has 2048. `latent_counts`: one segment has all 48 rows valid and one has 2.
All inputs are finite; a program needn't handle non-finite values.
Results may differ from a plain program's by a relative error of at most 0.019.
Values may be sent and summed in bfloat16 or wider, within the bound.
No kernel may reach another device: no remote copies, remote signals or barrier semaphores. Data moves between devices by JAX's collectives and lax.ppermute only.
A program may use at most 64 MiB of HBM per device.

v0:
```python
import math

import jax
import jax.numpy as jnp
from jax import lax
from jax.experimental import pallas as pl
from jax.experimental.pallas import tpu as pltpu
from jax.sharding import Mesh
from jax.sharding import PartitionSpec as P


MB = 128
HIDDEN = -1e30
GATE_ROWS = 8
NEAR = 4


def spread_kernel(gate_ref, query_ref, grad_ref, latent_key_ref, latent_value_ref, text_ref, packed_ref):
    peers, _, _, width = text_ref.shape
    for peer in range(peers):
        columns = pl.ds(peer * width, width)
        text_ref[peer, 0] = query_ref[:, columns]
        text_ref[peer, 1] = grad_ref[:, columns]

    @pl.when(pl.program_id(0) == 0)
    def _():
        slots, dim = latent_key_ref.shape
        packed_ref[:slots, :dim] = latent_key_ref[...]
        packed_ref[:slots, dim:] = latent_value_ref[...]
        gate = jnp.full((GATE_ROWS, 2 * dim), gate_ref[0], jnp.float32)
        first = gate.astype(jnp.bfloat16).astype(jnp.float32)
        second = (gate - first).astype(jnp.bfloat16).astype(jnp.float32)
        third = gate - first - second
        lane = lax.broadcasted_iota(jnp.int32, gate.shape, 1)
        terms = jnp.where(lane == 0, first, jnp.where(lane == 1, second, third))
        packed_ref[slots:, :] = jnp.where(lane < 3, terms, 0.0).astype(jnp.bfloat16)


def spread(gate_logits, queries, cotangent, latent_keys, latent_values, halves, peers):
    rows, columns = queries.shape
    width = columns // (halves * peers)
    slots, dim = latent_keys.shape
    parts = 2
    chunk = columns // (halves * parts)
    whole = pl.BlockSpec((slots, dim), lambda i: (0, 0))
    return pl.pallas_call(
        spread_kernel,
        grid=(halves * parts,),
        in_specs=[
            pl.BlockSpec(memory_space=pltpu.SMEM),
            pl.BlockSpec((rows, chunk), lambda i: (0, i)),
            pl.BlockSpec((rows, chunk), lambda i: (0, i)),
            whole,
            whole,
        ],
        out_specs=[
            pl.BlockSpec((peers // parts, 2, rows, width), lambda i: (i % parts, i // parts, 0, 0)),
            pl.BlockSpec((slots + GATE_ROWS, 2 * dim), lambda i: (0, 0)),
        ],
        out_shape=[
            jax.ShapeDtypeStruct((peers, 2 * halves, rows, width), queries.dtype),
            jax.ShapeDtypeStruct((slots + GATE_ROWS, 2 * dim), queries.dtype),
        ],
        name="spread",
        cost_estimate=pl.CostEstimate(
            flops=0, bytes_accessed=8 * rows * columns, transcendentals=0
        ),
    )(gate_logits, queries, cotangent, latent_keys, latent_values)


def collect_kernel(text_ref, mixed_ref, grad_ref):
    peers, _, _, width = text_ref.shape
    for peer in range(peers):
        columns = pl.ds(peer * width, width)
        mixed_ref[:, columns] = text_ref[peer, 0]
        grad_ref[:, columns] = text_ref[peer, 1]


def collect(text):
    peers, kinds, rows, width = text.shape
    halves = kinds // 2
    columns = halves * peers * width
    parts = 2
    whole = jax.ShapeDtypeStruct((rows, columns), text.dtype)
    block = pl.BlockSpec((rows, columns // (halves * parts)), lambda i: (0, i))
    return pl.pallas_call(
        collect_kernel,
        grid=(halves * parts,),
        in_specs=[
            pl.BlockSpec((peers // parts, 2, rows, width), lambda i: (i % parts, i // parts, 0, 0))
        ],
        out_specs=[block, block],
        out_shape=[whole, whole],
        name="collect",
        cost_estimate=pl.CostEstimate(
            flops=0, bytes_accessed=8 * rows * columns, transcendentals=0
        ),
    )(text)


def heads_kernel(
    place_ref,
    text_counts_ref,
    latent_counts_ref,
    latent_ref,
    visible_ref,
    text_ref,
    out_ref,
    keep_ref,
    send_ref,
    key_ref,
    value_ref,
    key_turned_ref,
    value_turned_ref,
    gate_ref,
    key_sum_ref,
    value_sum_ref,
):
    step = pl.program_id(1)
    steps = pl.num_programs(1)
    groups, _, rows, dim = text_ref.shape
    cores, pairs, seg_rows, _ = latent_ref.shape
    segments = cores * pairs
    slots = seg_rows - GATE_ROWS
    lanes = visible_ref.shape[1]
    block_rows = groups * rows
    scaling = 1.0 / math.sqrt(dim)
    to_power = scaling * math.log2(math.e)
    seg_index = place_ref[0] // 2
    half_index = place_ref[0] % 2

    @pl.when(step == 0)
    def _():
        for s in range(segments):
            at = pl.ds(s * slots, slots)
            latent = latent_ref.at[s % cores, s // cores]
            key_ref[at, :dim] = latent[:slots, :dim]
            value_ref[at, :] = latent[:slots, dim:]
            slot_ok = lax.broadcasted_iota(jnp.int32, (slots, lanes), 0) < latent_counts_ref[s]
            seen = jnp.broadcast_to(visible_ref[s : s + 1, :] > 0, (slots, lanes))
            key_ref[at, dim:] = jnp.where(slot_ok & seen, 0.0, HIDDEN).astype(jnp.bfloat16)
        key_turned_ref[...] = key_ref[:, :dim].astype(jnp.float32).T.astype(jnp.bfloat16)
        value_turned_ref[...] = value_ref[...].astype(jnp.float32).T.astype(jnp.bfloat16)
        terms = latent_ref[0, 0, slots:, :dim].astype(jnp.float32)[0:1, :]
        gate_ref[...] = jnp.tanh(jnp.broadcast_to(jnp.sum(terms, axis=1, keepdims=True), (1, dim)))
        key_sum_ref[...] = jnp.zeros_like(key_sum_ref)
        value_sum_ref[...] = jnp.zeros_like(value_sum_ref)

    own_count = text_counts_ref[seg_index] - half_index * (steps * block_rows)
    first_block = (place_ref[0] * (steps * groups)) % lanes
    first_row = step * block_rows
    gate = gate_ref[...]
    valid_column = (
        lax.broadcasted_iota(jnp.int32, (block_rows, dim), 0) + first_row < own_count
    )
    valid_row = (
        lax.broadcasted_iota(jnp.int32, (dim, block_rows), 1) + first_row < own_count
    )
    query = text_ref[:, 0].reshape(block_rows, dim)
    grad = text_ref[:, 1].reshape(block_rows, dim)
    grad_wide = jnp.where(valid_column, grad.astype(jnp.float32) * gate, 0.0)
    grad_out = grad_wide.astype(jnp.bfloat16)
    block_of = lax.broadcasted_iota(jnp.int32, (groups, rows, lanes), 0).reshape(block_rows, lanes)
    lane_of = lax.broadcasted_iota(jnp.int32, (block_rows, lanes), 1)
    pick = jnp.where(lane_of == block_of + (first_block + step * groups), 1.0, 0.0)
    asked = jnp.concatenate([query, pick.astype(jnp.bfloat16)], axis=1)
    turned = (((1,), (1,)), ((), ()))
    scores = lax.dot_general(key_ref[...], asked, turned, preferred_element_type=jnp.float32)
    top = jnp.max(scores, axis=0, keepdims=True)
    powers = jnp.exp2((scores - top) * to_power)
    total = jnp.sum(powers, axis=0, keepdims=True)
    weights = (powers * (1.0 / total)).astype(jnp.bfloat16)
    attended = jnp.dot(value_turned_ref[...], weights, preferred_element_type=jnp.float32)
    attended = attended.astype(jnp.bfloat16).astype(jnp.float32)
    mixed = jnp.where(valid_row, attended * gate[:, 0:1], 0.0)
    out_ref[:, 0] = mixed.T.astype(jnp.bfloat16).reshape(groups, rows, dim)
    grad_turned = grad_out.astype(jnp.float32).T
    delta = jnp.sum(grad_turned * attended, axis=0, keepdims=True)
    grad_weights = jnp.dot(
        value_ref[...], grad_turned.astype(jnp.bfloat16), preferred_element_type=jnp.float32
    )
    grad_scores = (weights.astype(jnp.float32) * (grad_weights - delta)).astype(jnp.bfloat16)
    grad_query = (
        jnp.dot(key_turned_ref[...], grad_scores, preferred_element_type=jnp.float32) * scaling
    )
    out_ref[:, 1] = grad_query.T.astype(jnp.bfloat16).reshape(groups, rows, dim)
    key_sum_ref[...] += jnp.dot(grad_scores, query, preferred_element_type=jnp.float32)
    value_sum_ref[...] += jnp.dot(weights, grad_out, preferred_element_type=jnp.float32)

    @pl.when(step == steps - 1)
    def _():
        core_index = seg_index % cores
        pair_index = seg_index // cores
        for near in range(NEAR):
            for far in range(pairs // NEAR):
                pair = pair_index ^ (far * NEAR + near)
                for ref, core in ((keep_ref, core_index), (send_ref, 1 - core_index)):
                    at = pl.ds(pl.multiple_of((pair * cores + core) * slots, 8), slots)
                    ref[near, far, :, :dim] = (key_sum_ref[at, :] * scaling).astype(ref.dtype)
                    ref[near, far, :, dim:] = value_sum_ref[at, :].astype(ref.dtype)


def attend_heads(place, text_counts, latent_counts, latents, visible_turned, text, groups):
    peers, kinds, rows, dim = text.shape
    halves = kinds // 2
    cores, _, pairs, seg_rows, _ = latents.shape
    slots = seg_rows - GATE_ROWS
    lat = cores * pairs * slots
    lanes = 128
    steps = peers // groups
    fars = pairs // NEAR
    text_spec = pl.BlockSpec((groups, 2, rows, dim), lambda h, i, *s: (i, h, 0, 0))
    sum_spec = pl.BlockSpec(
        (NEAR, fars, slots, 2 * dim), lambda h, i, p, *s: (0, h ^ (p[0] % 2), 0, 0)
    )
    grid_spec = pltpu.PrefetchScalarGridSpec(
        num_scalar_prefetch=3,
        grid=(halves, steps),
        in_specs=[
            pl.BlockSpec(
                (cores, pl.Squeezed(), pairs, seg_rows, 2 * dim),
                lambda h, i, *s: (0, h, 0, 0, 0),
            ),
            pl.BlockSpec(
                (cores * pairs, lanes), lambda h, i, p, *s: (0, p[0] * peers * rows // MB // lanes)
            ),
            text_spec,
        ],
        out_specs=[text_spec, sum_spec, sum_spec],
        scratch_shapes=[
            pltpu.VMEM((lat, dim + lanes), jnp.bfloat16),
            pltpu.VMEM((lat, dim), jnp.bfloat16),
            pltpu.VMEM((dim, lat), jnp.bfloat16),
            pltpu.VMEM((dim, lat), jnp.bfloat16),
            pltpu.VMEM((1, dim), jnp.float32),
            pltpu.VMEM((lat, dim), jnp.float32),
            pltpu.VMEM((lat, dim), jnp.float32),
        ],
    )
    sums = (NEAR, halves * fars, slots, 2 * dim)
    return pl.pallas_call(
        heads_kernel,
        grid_spec=grid_spec,
        out_shape=[
            jax.ShapeDtypeStruct(text.shape, jnp.bfloat16),
            jax.ShapeDtypeStruct(sums, jnp.float32),
            jax.ShapeDtypeStruct(sums, jnp.bfloat16),
        ],
        name="attend_heads",
        compiler_params=pltpu.CompilerParams(vmem_limit_bytes=48 << 20),
        cost_estimate=pl.CostEstimate(
            flops=12 * halves * peers * rows * lat * dim,
            bytes_accessed=8 * halves * peers * rows * dim,
            transcendentals=halves * peers * rows * lat,
        ),
    )(place, text_counts, latent_counts, latents, visible_turned, text)


def add_up(keep, send):
    fars = keep.shape[1] // 2
    pairs = lax.axis_size("z_lo")
    other = lax.ppermute(send, "core", [(0, 1), (1, 0)])
    keep = keep + other.astype(jnp.float32)
    send = keep[1:].astype(jnp.bfloat16)
    keep = keep[0]
    arrived = []
    for near in range(1, NEAR):
        steps = [(i, i ^ near) for i in range(pairs)]
        arrived.append(lax.ppermute(send[near - 1], "z_lo", steps))
    for other in arrived:
        keep = keep + other.astype(jnp.float32)
    other = lax.ppermute(keep[fars:].astype(jnp.bfloat16), "z_hi", [(0, 1), (1, 0)])
    keep = keep[:fars] + other.astype(jnp.float32)
    steps = [(i, i ^ NEAR) for i in range(pairs)]
    other = lax.ppermute(keep[1].astype(jnp.bfloat16), "z_lo", steps)
    return (keep[0] + other.astype(jnp.float32)).astype(jnp.bfloat16)


def shards(
    queries,
    latent_keys,
    latent_values,
    cotangent,
    gate_logits,
    visibility,
    text_counts,
    latent_counts,
):
    halves = lax.axis_size("z_hi")
    peers = lax.axis_size("x") * lax.axis_size("y")
    dim = latent_keys.shape[1]
    place = lax.axis_index(("z_lo", "core", "z_hi")).astype(jnp.int32).reshape(1)
    text, packed = spread(
        gate_logits, queries, cotangent, latent_keys, latent_values, halves, peers
    )
    text = lax.all_to_all(text, ("x", "y"), split_axis=0, concat_axis=0, tiled=True)
    latents = lax.all_gather(packed, ("z_hi", "z_lo"), axis=0, tiled=True)
    latents = lax.all_gather(latents, "core", axis=0, tiled=True)
    latents = latents.reshape(lax.axis_size("core"), halves, lax.axis_size("z_lo"), *packed.shape)
    out, keep, send = attend_heads(
        place, text_counts, latent_counts, latents, visibility.T, text, groups=4
    )
    out = lax.all_to_all(out, ("x", "y"), split_axis=0, concat_axis=0, tiled=True)
    grads = add_up(keep, send)
    mixed_rows, grad_queries = collect(out)
    return (mixed_rows, grad_queries, grads[:, :dim], grads[:, dim:])


def solution(mesh):
    fine = Mesh(mesh.devices.reshape(8, 2, 2, 4, 4), ("z_lo", "core", "z_hi", "x", "y"))
    seg, head = ("z_lo", "core"), ("z_hi", "x", "y")
    in_specs = (
        P(seg + head, None),
        P(seg, head),
        P(seg, head),
        P(seg + head, None),
        P(head),
        P(),
        P(),
        P(),
    )
    out_specs = (P(seg + head, None), P(seg + head, None), P(seg, head), P(seg, head))
    return jax.shard_map(shards, mesh=fine, in_specs=in_specs, out_specs=out_specs, check_vma=False)
```

profile of v0, /device:TPU:6, one launch (start us, length us, event | category | flops | bytes accessed | tf_op | source)
XLA Modules:
  0.0 127.6 jit_solution(15800955537087758953)
XLA Ops:
  1.3 4.0 %spread.1 = (bf16[16,4,128,128]{3,2,1,0:T(8,128)(2,1)}, bf16[56,256]{1,0:T(8,128)(2,1)}) custom-call(f32[1]{0:T(128)S(6)} %copy.12.gate_ref, bf16[128,4096]{1,0:T(8,128)(2,1)} %query_ref.1, bf16[128,4096]{1,0:T(8,128)(2,1)} %grad_ref.1, bf16[48,128]{1,0:T(8,128)(2,1)} %latent_key_ref.1, bf16[48,128]{1,0:T(8,128)(2,1)} %latent_value_ref.1), custom_call_target="tpu_custom_call" | custom-call | bytes 4194304 | tf_op jit(solution)/shard_map/spread/pallas_call | solution.py:46
  5.2 0.0 copy-start.3
  5.2 0.0 copy-start
  5.2 0.0 copy-start.1
  5.3 0.0 copy-start.2
  5.3 10.2 %all-to-all-start = ((bf16[16,4,128,128]{3,2,1,0:T(8,128)(2,1)}), bf16[16,4,128,128]{3,2,1,0:T(8,128)(2,1)}, u32[]{:S(2)}, u32[]{:S(2)}) async-start(bf16[16,4,128,128]{3,2,1,0:T(8,128)(2,1)} %get-tuple-element.12), calls=%async_computation | async-start | bytes 4194304 | tf_op jit(solution)/shard_map/all_to_all | solution.py:296
  15.5 0.0 copy-done.3
  15.5 35.3 %all_gather.6 = bf16[896,256]{1,0:T(8,128)(2,1)S(1)} all-gather(bf16[56,256]{1,0:T(8,128)(2,1)S(1)} %copy-done.3), channel_id=1, replica_groups=mesh['z_lo'=8,'core'=2,'z_hi'=2,'x'=4,'y'=4] {'z_hi','z_lo'}, dimensions={0}, use_global_device_ids=true | all-gather | bytes 487424 | tf_op jit(solution)/shard_map/all_gather | solution.py:297
  50.8 2.5 %all_gather.7 = bf16[1792,256]{1,0:T(8,128)(2,1)S(1)} all-gather(bf16[896,256]{1,0:T(8,128)(2,1)S(1)} %all_gather.6), channel_id=1, replica_groups=mesh['z_lo'=8,'core'=2,'z_hi'=2,'x'=4,'y'=4] {'core'}, dimensions={0}, use_global_device_ids=true | all-gather | bytes 1376256 | tf_op jit(solution)/shard_map/all_gather | solution.py:298
  53.3 0.0 all-to-all-done.text_ref
  53.3 0.0 copy-done
  53.3 0.0 copy-done.1
  53.3 0.0 copy-done.2
  53.3 18.4 %attend_heads.1 = (bf16[16,4,128,128]{3,2,1,0:T(8,128)(2,1)}, f32[4,4,48,256]{3,2,1,0:T(8,128)S(1)}, bf16[4,4,48,256]{3,2,1,0:T(8,128)(2,1)S(1)}) custom-call(s32[1]{0:T(128)} %bitcast.place_ref, s32[16]{0:T(128)S(1)} %copy-done.1, s32[16]{0:T(128)S(1)} %copy-done.2, bf16[2,2,8,56,256]{4,3,2,1,0:T(8,128)(2,1)S(1)} %bitcast.25, s32[16,512]{1,0:T(8,128)S(1)} %bitcast.26, ...), custom_call_target="tpu_custom_call" | custom-call | flops 4831838208 | bytes 4194304 | tf_op jit(solution)/shard_map/attend_heads/pallas_call | solution.py:241
  71.7 2.0 %collective-permute-start = (bf16[4,4,48,256]{3,2,1,0:T(8,128)(2,1)S(1)}, bf16[4,4,48,256]{3,2,1,0:T(8,128)(2,1)S(1)}, u32[]{:S(2)}, u32[]{:S(2)}) collective-permute-start(bf16[4,4,48,256]{3,2,1,0:T(8,128)(2,1)S(1)} %get-tuple-element.17), channel_id=1, source_target_pairs={{0,32},{32,0},{1,33},{33,1},{2,34},{34,2},{3,35},{35,3},{4,36},{36... | collective-permute-start | bytes 1179656 | tf_op jit(solution)/shard_map/ppermute | solution.py:262
  73.8 7.2 %all-to-all-start.1 = ((bf16[16,4,128,128]{3,2,1,0:T(8,128)(2,1)}), bf16[16,4,128,128]{3,2,1,0:T(8,128)(2,1)}, u32[]{:S(2)}, u32[]{:S(2)}) async-start(bf16[16,4,128,128]{3,2,1,0:T(8,128)(2,1)} %get-tuple-element.13), calls=%async_computation.1 | async-start | bytes 4194304 | tf_op jit(solution)/shard_map/all_to_all | solution.py:303
  81.0 0.0 collective-permute-done
  81.0 0.1 fusion.6
  81.2 1.9 %collective-permute-start.1 = (bf16[4,48,256]{2,1,0:T(8,128)(2,1)S(1)}, bf16[4,48,256]{2,1,0:T(8,128)(2,1)S(1)}, u32[]{:S(2)}, u32[]{:S(2)}) collective-permute-start(bf16[4,48,256]{2,1,0:T(8,128)(2,1)S(1)} %get-tuple-element.20), channel_id=1, source_target_pairs={{0,64},{64,0},{128,192},{192,128},{256,320},{320,256},{384,448},{4... | collective-permute-start | bytes 294920 | tf_op jit(solution)/shard_map/ppermute | solution.py:269
  83.1 3.6 %collective-permute-start.3 = (bf16[4,48,256]{2,1,0:T(8,128)(2,1)S(1)}, bf16[4,48,256]{2,1,0:T(8,128)(2,1)S(1)}, u32[]{:S(2)}, u32[]{:S(2)}) collective-permute-start(bf16[4,48,256]{2,1,0:T(8,128)(2,1)S(1)} %get-tuple-element.21), channel_id=1, source_target_pairs={{0,192},{64,128},{128,64},{192,0},{256,448},{320,384},{384,320},{4... | collective-permute-start | bytes 294920 | tf_op jit(solution)/shard_map/ppermute | solution.py:269
  86.7 3.7 %collective-permute-start.2 = (bf16[4,48,256]{2,1,0:T(8,128)(2,1)S(1)}, bf16[4,48,256]{2,1,0:T(8,128)(2,1)S(1)}, u32[]{:S(2)}, u32[]{:S(2)}) collective-permute-start(bf16[4,48,256]{2,1,0:T(8,128)(2,1)S(1)} %get-tuple-element.22), channel_id=1, source_target_pairs={{0,128},{64,192},{128,0},{192,64},{256,384},{320,448},{384,256},{4... | collective-permute-start | bytes 294920 | tf_op jit(solution)/shard_map/ppermute | solution.py:269
  90.4 0.0 collective-permute-done.1
  90.4 1.0 collective-permute-done.3
  91.4 5.6 %collective-permute-done.2 = bf16[4,48,256]{2,1,0:T(8,128)(2,1)S(1)} collective-permute-done((bf16[4,48,256]{2,1,0:T(8,128)(2,1)S(1)}, bf16[4,48,256]{2,1,0:T(8,128)(2,1)S(1)}, u32[]{:S(2)}, u32[]{:S(2)}) %collective-permute-start.2) | collective-permute-done | bytes 98336 | tf_op jit(solution)/shard_map/ppermute | solution.py:269
  97.1 7.5 %collective-permute-start.4 = (bf16[2,48,256]{2,1,0:T(8,128)(2,1)S(1)}, bf16[2,48,256]{2,1,0:T(8,128)(2,1)S(1)}, u32[]{:S(2)}, u32[]{:S(2)}) collective-permute-start(bf16[2,48,256]{2,1,0:T(8,128)(2,1)S(1)} %slice.77), channel_id=1, source_target_pairs={{0,16},{16,0},{1,17},{17,1},{2,18},{18,2},{3,19},{19,3},{4,20},{20... | collective-permute-start | bytes 147464 | tf_op jit(solution)/shard_map/ppermute | solution.py:272
  104.6 8.7 %collective-permute-done.4 = bf16[2,48,256]{2,1,0:T(8,128)(2,1)S(1)} collective-permute-done((bf16[2,48,256]{2,1,0:T(8,128)(2,1)S(1)}, bf16[2,48,256]{2,1,0:T(8,128)(2,1)S(1)}, u32[]{:S(2)}, u32[]{:S(2)}) %collective-permute-start.4) | collective-permute-done | bytes 49184 | tf_op jit(solution)/shard_map/ppermute | solution.py:272
  113.4 2.0 %collective-permute-start.5 = (bf16[48,256]{1,0:T(8,128)(2,1)S(1)}, bf16[48,256]{1,0:T(8,128)(2,1)S(1)}, u32[]{:S(2)}, u32[]{:S(2)}) collective-permute-start(bf16[48,256]{1,0:T(8,128)(2,1)S(1)} %fusion.5), channel_id=1, source_target_pairs={{0,256},{64,320},{128,384},{192,448},{256,0},{320,64},{384,128},{4... | collective-permute-start | bytes 73736 | tf_op jit(solution)/shard_map/ppermute | solution.py:275
  115.4 7.6 %collective-permute-done.5 = bf16[48,256]{1,0:T(8,128)(2,1)S(1)} collective-permute-done((bf16[48,256]{1,0:T(8,128)(2,1)S(1)}, bf16[48,256]{1,0:T(8,128)(2,1)S(1)}, u32[]{:S(2)}, u32[]{:S(2)}) %collective-permute-start.5) | collective-permute-done | bytes 24608 | tf_op jit(solution)/shard_map/ppermute | solution.py:275
  123.0 0.6 fusion.7
  123.6 0.0 all-to-all-done.1.text_ref
  123.6 4.0 %collect.1 = (bf16[128,4096]{1,0:T(8,128)(2,1)}, bf16[128,4096]{1,0:T(8,128)(2,1)}) custom-call(bf16[16,4,128,128]{3,2,1,0:T(8,128)(2,1)} %all-to-all-done.1.text_ref), custom_call_target="tpu_custom_call" | custom-call | bytes 4194304 | tf_op jit(solution)/shard_map/collect/pallas_call | solution.py:86
  (6 shorter events, 0.1 us)
Async XLA Ops:
  5.2 10.2 %copy-start.3 = (bf16[56,256]{1,0:T(8,128)(2,1)S(1)}, bf16[56,256]{1,0:T(8,128)(2,1)}, u32[]{:S(2)}) copy-start(bf16[56,256]{1,0:T(8,128)(2,1)} %get-tuple-element.11) | copy-start | bytes 86020
  5.2 48.0 %copy-start = (s32[512,16]{0,1:T(8,128)S(1)}, s32[512,16]{0,1:T(8,128)}, u32[]{:S(2)}) copy-start(s32[512,16]{0,1:T(8,128)} %param.13) | copy-start | bytes 98308
  5.2 48.0 %copy-start.1 = (s32[16]{0:T(128)S(1)}, s32[16]{0:T(128)}, u32[]{:S(2)}) copy-start(s32[16]{0:T(128)} %text_counts_ref.1) | copy-start | bytes 196
  5.3 48.0 %copy-start.2 = (s32[16]{0:T(128)S(1)}, s32[16]{0:T(128)}, u32[]{:S(2)}) copy-start(s32[16]{0:T(128)} %latent_counts_ref.1) | copy-start | bytes 196
  5.3 48.0 %all-to-all-start = ((bf16[16,4,128,128]{3,2,1,0:T(8,128)(2,1)}), bf16[16,4,128,128]{3,2,1,0:T(8,128)(2,1)}, u32[]{:S(2)}, u32[]{:S(2)}) async-start(bf16[16,4,128,128]{3,2,1,0:T(8,128)(2,1)} %get-tuple-element.12), calls=%async_computation | async-start | bytes 4194304 | tf_op jit(solution)/shard_map/all_to_all | solution.py:296
  71.7 9.3 %collective-permute-start = (bf16[4,4,48,256]{3,2,1,0:T(8,128)(2,1)S(1)}, bf16[4,4,48,256]{3,2,1,0:T(8,128)(2,1)S(1)}, u32[]{:S(2)}, u32[]{:S(2)}) collective-permute-start(bf16[4,4,48,256]{3,2,1,0:T(8,128)(2,1)S(1)} %get-tuple-element.17), channel_id=1, source_target_pairs={{0,32},{32,0},{1,33},{33,1},{2,34},{34,2},{3,35},{35,3},{4,36},{36... | collective-permute-start | bytes 1179656 | tf_op jit(solution)/shard_map/ppermute | solution.py:262
  73.8 49.9 %all-to-all-start.1 = ((bf16[16,4,128,128]{3,2,1,0:T(8,128)(2,1)}), bf16[16,4,128,128]{3,2,1,0:T(8,128)(2,1)}, u32[]{:S(2)}, u32[]{:S(2)}) async-start(bf16[16,4,128,128]{3,2,1,0:T(8,128)(2,1)} %get-tuple-element.13), calls=%async_computation.1 | async-start | bytes 4194304 | tf_op jit(solution)/shard_map/all_to_all | solution.py:303
  81.2 9.2 %collective-permute-start.1 = (bf16[4,48,256]{2,1,0:T(8,128)(2,1)S(1)}, bf16[4,48,256]{2,1,0:T(8,128)(2,1)S(1)}, u32[]{:S(2)}, u32[]{:S(2)}) collective-permute-start(bf16[4,48,256]{2,1,0:T(8,128)(2,1)S(1)} %get-tuple-element.20), channel_id=1, source_target_pairs={{0,64},{64,0},{128,192},{192,128},{256,320},{320,256},{384,448},{4... | collective-permute-start | bytes 294920 | tf_op jit(solution)/shard_map/ppermute | solution.py:269
  83.1 8.3 %collective-permute-start.3 = (bf16[4,48,256]{2,1,0:T(8,128)(2,1)S(1)}, bf16[4,48,256]{2,1,0:T(8,128)(2,1)S(1)}, u32[]{:S(2)}, u32[]{:S(2)}) collective-permute-start(bf16[4,48,256]{2,1,0:T(8,128)(2,1)S(1)} %get-tuple-element.21), channel_id=1, source_target_pairs={{0,192},{64,128},{128,64},{192,0},{256,448},{320,384},{384,320},{4... | collective-permute-start | bytes 294920 | tf_op jit(solution)/shard_map/ppermute | solution.py:269
  86.7 10.3 %collective-permute-start.2 = (bf16[4,48,256]{2,1,0:T(8,128)(2,1)S(1)}, bf16[4,48,256]{2,1,0:T(8,128)(2,1)S(1)}, u32[]{:S(2)}, u32[]{:S(2)}) collective-permute-start(bf16[4,48,256]{2,1,0:T(8,128)(2,1)S(1)} %get-tuple-element.22), channel_id=1, source_target_pairs={{0,128},{64,192},{128,0},{192,64},{256,384},{320,448},{384,256},{4... | collective-permute-start | bytes 294920 | tf_op jit(solution)/shard_map/ppermute | solution.py:269
  97.1 16.3 %collective-permute-start.4 = (bf16[2,48,256]{2,1,0:T(8,128)(2,1)S(1)}, bf16[2,48,256]{2,1,0:T(8,128)(2,1)S(1)}, u32[]{:S(2)}, u32[]{:S(2)}) collective-permute-start(bf16[2,48,256]{2,1,0:T(8,128)(2,1)S(1)} %slice.77), channel_id=1, source_target_pairs={{0,16},{16,0},{1,17},{17,1},{2,18},{18,2},{3,19},{19,3},{4,20},{20... | collective-permute-start | bytes 147464 | tf_op jit(solution)/shard_map/ppermute | solution.py:272
  113.4 9.6 %collective-permute-start.5 = (bf16[48,256]{1,0:T(8,128)(2,1)S(1)}, bf16[48,256]{1,0:T(8,128)(2,1)S(1)}, u32[]{:S(2)}, u32[]{:S(2)}) collective-permute-start(bf16[48,256]{1,0:T(8,128)(2,1)S(1)} %fusion.5), channel_id=1, source_target_pairs={{0,256},{64,320},{128,384},{192,448},{256,0},{320,64},{384,128},{4... | collective-permute-start | bytes 73736 | tf_op jit(solution)/shard_map/ppermute | solution.py:275
where the time goes:
time: 128 us
  starting transfers between devices  38.2 us (30%)
  blocking collectives  37.8 us (30%)
  Pallas kernels  26.4 us (21%)
  waiting for transfers between devices  22.9 us (18%)
  between operations  1.42 us (1%)
    all_gather x1, blocking collectives, shards(): latents = lax.all_gather(packed, ('z_hi', 'z_lo'), axis=0, tiled=True)  35.3 us
    pallas_call x1, Pallas kernels, attend_heads(): pl.pallas_call(heads_kernel, grid_spec=grid_spec, out_shape=[jax.ShapeDty...  18.4 us
    all_to_all x1, starting transfers between devices, shards(): lax.all_to_all(text, ('x', 'y'), split_axis=0, concat_axis=0, tiled=True)  10.2 us
    ppermute x3, starting transfers between devices, add_up(): arrived.append(lax.ppermute(send[near - 1], 'z_lo', steps))  9.21 us
    ppermute x1, waiting for transfers between devices, add_up(): lax.ppermute(keep[fars:].astype(jnp.bfloat16), 'z_hi', [(0, 1), (1, 0)])  8.73 us
    ppermute x1, waiting for transfers between devices, add_up(): other = lax.ppermute(keep[1].astype(jnp.bfloat16), 'z_lo', steps)  7.6 us
    ppermute x1, starting transfers between devices, add_up(): lax.ppermute(keep[fars:].astype(jnp.bfloat16), 'z_hi', [(0, 1), (1, 0)])  7.54 us
    all_to_all x1, starting transfers between devices, shards(): lax.all_to_all(out, ('x', 'y'), split_axis=0, concat_axis=0, tiled=True)  7.23 us
  transfers between devices with their start and end apart: 8, of which 4 were waited for; matrix products, arithmetic and copies ran while one was open for 1% of the time, Pallas kernels for 0%

commit v1 on v0

--- a/solution.py
+++ b/solution.py
@@ -15,81 +15,102 @@
 NEAR = 4
 
 
-def spread_kernel(gate_ref, query_ref, grad_ref, latent_key_ref, latent_value_ref, text_ref, packed_ref):
-    peers, _, _, width = text_ref.shape
-    for peer in range(peers):
-        columns = pl.ds(peer * width, width)
-        text_ref[peer, 0] = query_ref[:, columns]
-        text_ref[peer, 1] = grad_ref[:, columns]
-
-    @pl.when(pl.program_id(0) == 0)
-    def _():
-        slots, dim = latent_key_ref.shape
-        packed_ref[:slots, :dim] = latent_key_ref[...]
-        packed_ref[:slots, dim:] = latent_value_ref[...]
-        gate = jnp.full((GATE_ROWS, 2 * dim), gate_ref[0], jnp.float32)
-        first = gate.astype(jnp.bfloat16).astype(jnp.float32)
-        second = (gate - first).astype(jnp.bfloat16).astype(jnp.float32)
-        third = gate - first - second
-        lane = lax.broadcasted_iota(jnp.int32, gate.shape, 1)
-        terms = jnp.where(lane == 0, first, jnp.where(lane == 1, second, third))
-        packed_ref[slots:, :] = jnp.where(lane < 3, terms, 0.0).astype(jnp.bfloat16)
+def spread_kernel(
+    gate_ref,
+    latent_key_ref,
+    latent_value_ref,
+    query_ref,
+    grad_ref,
+    text_ref,
+    packed_ref,
+    held_ref,
+    in_sems,
+    out_sems,
+):
+    peers, kinds, _, width = text_ref.shape
+    halves = kinds // 2
+    chunks = in_sems.shape[1]
+    chunk = query_ref.shape[1] // chunks
+    chunk_peers = halves * peers // chunks
+
+    def bring(kind, c):
+        columns = pl.ds(c * chunk, chunk)
+        source = (query_ref, grad_ref)[kind].at[:, columns]
+        return pltpu.make_async_copy(source, held_ref.at[kind, :, columns], in_sems.at[kind, c])
+
+    def put(kind, head):
+        half, peer = head // peers, head % peers
+        return pltpu.make_async_copy(
+            held_ref.at[kind, :, pl.ds(head * width, width)],
+            text_ref.at[peer, 2 * half + kind],
+            out_sems.at[kind, head],
+        )
+
+    for c in range(chunks):
+        for kind in range(2):
+            bring(kind, c).start()
+    slots, dim = latent_key_ref.shape
+    packed_ref[:slots, :dim] = latent_key_ref[...]
+    packed_ref[:slots, dim:] = latent_value_ref[...]
+    gate = jnp.full((GATE_ROWS, 2 * dim), gate_ref[0], jnp.float32)
+    first = gate.astype(jnp.bfloat16).astype(jnp.float32)
+    second = (gate - first).astype(jnp.bfloat16).astype(jnp.float32)
+    third = gate - first - second
+    lane = lax.broadcasted_iota(jnp.int32, gate.shape, 1)
+    terms = jnp.where(lane == 0, first, jnp.where(lane == 1, second, third))
+    packed_ref[slots:, :] = jnp.where(lane < 3, terms, 0.0).astype(jnp.bfloat16)
+    for c in range(chunks):
+        for kind in range(2):
+            bring(kind, c).wait()
+            for head in range(c * chunk_peers, (c + 1) * chunk_peers):
+                put(kind, head).start()
+    for head in range(halves * peers):
+        for kind in range(2):
+            put(kind, head).wait()
 
 
 def spread(gate_logits, queries, cotangent, latent_keys, latent_values, halves, peers):
     rows, columns = queries.shape
     width = columns // (halves * peers)
     slots, dim = latent_keys.shape
-    parts = 2
-    chunk = columns // (halves * parts)
-    whole = pl.BlockSpec((slots, dim), lambda i: (0, 0))
+    chunks = 4
+    vmem = pl.BlockSpec(memory_space=pltpu.VMEM)
+    anywhere = pl.BlockSpec(memory_space=pl.ANY)
     return pl.pallas_call(
         spread_kernel,
-        grid=(halves * parts,),
-        in_specs=[
-            pl.BlockSpec(memory_space=pltpu.SMEM),
-            pl.BlockSpec((rows, chunk), lambda i: (0, i)),
-            pl.BlockSpec((rows, chunk), lambda i: (0, i)),
-            whole,
-            whole,
-        ],
-        out_specs=[
-            pl.BlockSpec((peers // parts, 2, rows, width), lambda i: (i % parts, i // parts, 0, 0)),
-            pl.BlockSpec((slots + GATE_ROWS, 2 * dim), lambda i: (0, 0)),
-        ],
+        in_specs=[pl.BlockSpec(memory_space=pltpu.SMEM), vmem, vmem, anywhere, anywhere],
+        out_specs=[anywhere, vmem],
         out_shape=[
             jax.ShapeDtypeStruct((peers, 2 * halves, rows, width), queries.dtype),
             jax.ShapeDtypeStruct((slots + GATE_ROWS, 2 * dim), queries.dtype),
+        ],
+        scratch_shapes=[
+            pltpu.VMEM((2, rows, columns), queries.dtype),
+            pltpu.SemaphoreType.DMA((2, chunks)),
+            pltpu.SemaphoreType.DMA((2, halves * peers)),
         ],
         name="spread",
         cost_estimate=pl.CostEstimate(
             flops=0, bytes_accessed=8 * rows * columns, transcendentals=0
         ),
-    )(gate_logits, queries, cotangent, latent_keys, latent_values)
+    )(gate_logits, latent_keys, latent_values, queries, cotangent)
 
 
 def collect_kernel(text_ref, mixed_ref, grad_ref):
-    peers, _, _, width = text_ref.shape
-    for peer in range(peers):
-        columns = pl.ds(peer * width, width)
-        mixed_ref[:, columns] = text_ref[peer, 0]
-        grad_ref[:, columns] = text_ref[peer, 1]
+    peers, kinds, _, width = text_ref.shape
+    for half in range(kinds // 2):
+        for peer in range(peers):
+            columns = pl.ds((half * peers + peer) * width, width)
+            mixed_ref[:, columns] = text_ref[peer, 2 * half]
+            grad_ref[:, columns] = text_ref[peer, 2 * half + 1]
 
 
 def collect(text):
     peers, kinds, rows, width = text.shape
-    halves = kinds // 2
-    columns = halves * peers * width
-    parts = 2
+    columns = kinds // 2 * peers * width
     whole = jax.ShapeDtypeStruct((rows, columns), text.dtype)
-    block = pl.BlockSpec((rows, columns // (halves * parts)), lambda i: (0, i))
     return pl.pallas_call(
         collect_kernel,
-        grid=(halves * parts,),
-        in_specs=[
-            pl.BlockSpec((peers // parts, 2, rows, width), lambda i: (i % parts, i // parts, 0, 0))
-        ],
-        out_specs=[block, block],
         out_shape=[whole, whole],
         name="collect",
         cost_estimate=pl.CostEstimate(
@@ -269,11 +290,18 @@
         arrived.append(lax.ppermute(send[near - 1], "z_lo", steps))
     for other in arrived:
         keep = keep + other.astype(jnp.float32)
-    other = lax.ppermute(keep[fars:].astype(jnp.bfloat16), "z_hi", [(0, 1), (1, 0)])
-    keep = keep[:fars] + other.astype(jnp.float32)
-    steps = [(i, i ^ NEAR) for i in range(pairs)]
-    other = lax.ppermute(keep[1].astype(jnp.bfloat16), "z_lo", steps)
-    return (keep[0] + other.astype(jnp.float32)).astype(jnp.bfloat16)
+    send = keep[1:].astype(jnp.bfloat16)
+    arrived = []
+    for far in (2, 1, 3):
+        half, block = far // fars, far % fars
+        steps = [
+            (2 * i + h, 2 * (i ^ (block * NEAR)) + (h ^ half)) for i in range(pairs) for h in range(2)
+        ]
+        arrived.append(lax.ppermute(send[far - 1], ("z_lo", "z_hi"), steps))
+    keep = keep[0]
+    for other in arrived:
+        keep = keep + other.astype(jnp.float32)
+    return keep.astype(jnp.bfloat16)
 
 
 def shards(

time: 128 us -> 125 us (0.977)
  waiting for transfers between devices: 22.9 us -> 12.3 us
  starting transfers between devices: 38.2 us -> 45.6 us
    ppermute x2 -> x3, waiting for transfers between devices: 16.3 us -> 3.69 us  [add_up(): arrived.append(lax.ppermute(send[far - 1], ('z_lo', 'z_hi'), steps))]
    ppermute x2 -> x3, starting transfers between devices: 9.56 us -> 17 us  [add_up(): arrived.append(lax.ppermute(send[far - 1], ('z_lo', 'z_hi'), steps))]
    ppermute x1, waiting for transfers between devices: 0.01 us -> 1.69 us  [add_up(): other = lax.ppermute(send, 'core', [(0, 1), (1, 0)])]
  transfers between devices with their start and end apart: 8 -> 9, of which waited for: 4 -> 4; matrix products, arithmetic and copies ran while one was open for 1% -> 1% of each run, Pallas kernels for 0% -> 0%
where the time goes in v1:
time: 125 us; the launch traced here: 124 us
  starting transfers between devices  45.6 us (36%)
  blocking collectives  37.8 us (30%)
  Pallas kernels  26.2 us (21%)
  waiting for transfers between devices  12.3 us (10%)
  between operations  1.45 us (1%)
    all_gather x1, blocking collectives, shards(): latents = lax.all_gather(packed, ('z_hi', 'z_lo'), axis=0, tiled=True)  35.4 us
    pallas_call x1, Pallas kernels, attend_heads(): pl.pallas_call(heads_kernel, grid_spec=grid_spec, out_shape=[jax.ShapeDty...  18.4 us
    ppermute x3, starting transfers between devices, add_up(): arrived.append(lax.ppermute(send[far - 1], ('z_lo', 'z_hi'), steps))  17 us
    all_to_all x1, starting transfers between devices, shards(): lax.all_to_all(text, ('x', 'y'), split_axis=0, concat_axis=0, tiled=True)  10.2 us
    ppermute x3, starting transfers between devices, add_up(): arrived.append(lax.ppermute(send[near - 1], 'z_lo', steps))  9.21 us
    all_to_all x1, starting transfers between devices, shards(): lax.all_to_all(out, ('x', 'y'), split_axis=0, concat_axis=0, tiled=True)  7.23 us
    ppermute x3, waiting for transfers between devices, add_up(): arrived.append(lax.ppermute(send[near - 1], 'z_lo', steps))  6.9 us
    pallas_call x1, Pallas kernels, spread(): pl.pallas_call(spread_kernel, in_specs=[pl.BlockSpec(memory_space=pltpu.S...  4.25 us
  transfers between devices with their start and end apart: 9, of which 4 were waited for; matrix products, arithmetic and copies ran while one was open for 1% of the time, Pallas kernels for 0%

profile of v1, /device:TPU:6, one launch (start us, length us, event | category | flops | bytes accessed | tf_op | source)
XLA Modules:
  0.0 124.2 jit_solution(879119513677067588)
XLA Ops:
  1.3 4.3 %spread.1 = (bf16[16,4,128,128]{3,2,1,0:T(8,128)(2,1)}, bf16[56,256]{1,0:T(8,128)(2,1)}) custom-call(f32[1]{0:T(128)S(6)} %copy.12.gate_ref, bf16[48,128]{1,0:T(8,128)(2,1)} %latent_key_ref.1, bf16[48,128]{1,0:T(8,128)(2,1)} %latent_value_ref.1, bf16[128,4096]{1,0:T(8,128)(2,1)} %query_ref.1, bf16[128,4096]{1,0:T(8,128)(2,1)} %grad_ref.1), custom_call_target="tpu_custom_call" | custom-call | bytes 4194304 | tf_op jit(solution)/shard_map/spread/pallas_call | solution.py:79
  5.5 0.0 copy-start.3
  5.6 0.0 copy-start
  5.6 0.0 copy-start.1
  5.6 0.0 copy-start.2
  5.6 10.2 %all-to-all-start = ((bf16[16,4,128,128]{3,2,1,0:T(8,128)(2,1)}), bf16[16,4,128,128]{3,2,1,0:T(8,128)(2,1)}, u32[]{:S(2)}, u32[]{:S(2)}) async-start(bf16[16,4,128,128]{3,2,1,0:T(8,128)(2,1)} %get-tuple-element.12), calls=%async_computation | async-start | bytes 4194304 | tf_op jit(solution)/shard_map/all_to_all | solution.py:324
  15.8 0.0 copy-done.3
  15.8 35.4 %all_gather.6 = bf16[896,256]{1,0:T(8,128)(2,1)S(1)} all-gather(bf16[56,256]{1,0:T(8,128)(2,1)S(1)} %copy-done.3), channel_id=1, replica_groups=mesh['z_lo'=8,'core'=2,'z_hi'=2,'x'=4,'y'=4] {'z_hi','z_lo'}, dimensions={0}, use_global_device_ids=true | all-gather | bytes 487424 | tf_op jit(solution)/shard_map/all_gather | solution.py:325
  51.2 2.5 %all_gather.7 = bf16[1792,256]{1,0:T(8,128)(2,1)S(1)} all-gather(bf16[896,256]{1,0:T(8,128)(2,1)S(1)} %all_gather.6), channel_id=1, replica_groups=mesh['z_lo'=8,'core'=2,'z_hi'=2,'x'=4,'y'=4] {'core'}, dimensions={0}, use_global_device_ids=true | all-gather | bytes 1376256 | tf_op jit(solution)/shard_map/all_gather | solution.py:326
  53.6 0.0 all-to-all-done.text_ref
  53.6 0.0 copy-done
  53.6 0.0 copy-done.1
  53.6 0.0 copy-done.2
  53.6 18.4 %attend_heads.1 = (bf16[16,4,128,128]{3,2,1,0:T(8,128)(2,1)}, f32[4,4,48,256]{3,2,1,0:T(8,128)S(1)}, bf16[4,4,48,256]{3,2,1,0:T(8,128)(2,1)S(1)}) custom-call(s32[1]{0:T(128)} %bitcast.place_ref, s32[16]{0:T(128)S(1)} %copy-done.1, s32[16]{0:T(128)S(1)} %copy-done.2, bf16[2,2,8,56,256]{4,3,2,1,0:T(8,128)(2,1)S(1)} %bitcast.34, s32[16,512]{1,0:T(8,128)S(1)} %bitcast.35, ...), custom_call_target="tpu_custom_call" | custom-call | flops 4831838208 | bytes 4194304 | tf_op jit(solution)/shard_map/attend_heads/pallas_call | solution.py:262
  72.1 7.2 %all-to-all-start.1 = ((bf16[16,4,128,128]{3,2,1,0:T(8,128)(2,1)}), bf16[16,4,128,128]{3,2,1,0:T(8,128)(2,1)}, u32[]{:S(2)}, u32[]{:S(2)}) async-start(bf16[16,4,128,128]{3,2,1,0:T(8,128)(2,1)} %get-tuple-element.13), calls=%async_computation.1 | async-start | bytes 4194304 | tf_op jit(solution)/shard_map/all_to_all | solution.py:331
  79.3 1.9 %collective-permute-start = (bf16[4,4,48,256]{3,2,1,0:T(8,128)(2,1)S(1)}, bf16[4,4,48,256]{3,2,1,0:T(8,128)(2,1)S(1)}, u32[]{:S(2)}, u32[]{:S(2)}) collective-permute-start(bf16[4,4,48,256]{3,2,1,0:T(8,128)(2,1)S(1)} %get-tuple-element.17), channel_id=1, source_target_pairs={{0,32},{32,0},{1,33},{33,1},{2,34},{34,2},{3,35},{35,3},{4,36},{36... | collective-permute-start | bytes 1179656 | tf_op jit(solution)/shard_map/ppermute | solution.py:283
  81.2 1.7 %collective-permute-done = bf16[4,4,48,256]{3,2,1,0:T(8,128)(2,1)S(1)} collective-permute-done((bf16[4,4,48,256]{3,2,1,0:T(8,128)(2,1)S(1)}, bf16[4,4,48,256]{3,2,1,0:T(8,128)(2,1)S(1)}, u32[]{:S(2)}, u32[]{:S(2)}) %collective-permute-start) | collective-permute-done | bytes 393248 | tf_op jit(solution)/shard_map/ppermute | solution.py:283
  82.9 0.1 fusion.9
  83.1 1.9 %collective-permute-start.1 = (bf16[4,48,256]{2,1,0:T(8,128)(2,1)S(1)}, bf16[4,48,256]{2,1,0:T(8,128)(2,1)S(1)}, u32[]{:S(2)}, u32[]{:S(2)}) collective-permute-start(bf16[4,48,256]{2,1,0:T(8,128)(2,1)S(1)} %get-tuple-element.22), channel_id=1, source_target_pairs={{0,64},{64,0},{128,192},{192,128},{256,320},{320,256},{384,448},{4... | collective-permute-start | bytes 294920 | tf_op jit(solution)/shard_map/ppermute | solution.py:290
  85.0 3.6 %collective-permute-start.3 = (bf16[4,48,256]{2,1,0:T(8,128)(2,1)S(1)}, bf16[4,48,256]{2,1,0:T(8,128)(2,1)S(1)}, u32[]{:S(2)}, u32[]{:S(2)}) collective-permute-start(bf16[4,48,256]{2,1,0:T(8,128)(2,1)S(1)} %get-tuple-element.23), channel_id=1, source_target_pairs={{0,192},{64,128},{128,64},{192,0},{256,448},{320,384},{384,320},{4... | collective-permute-start | bytes 294920 | tf_op jit(solution)/shard_map/ppermute | solution.py:290
  88.6 3.7 %collective-permute-start.2 = (bf16[4,48,256]{2,1,0:T(8,128)(2,1)S(1)}, bf16[4,48,256]{2,1,0:T(8,128)(2,1)S(1)}, u32[]{:S(2)}, u32[]{:S(2)}) collective-permute-start(bf16[4,48,256]{2,1,0:T(8,128)(2,1)S(1)} %get-tuple-element.24), channel_id=1, source_target_pairs={{0,128},{64,192},{128,0},{192,64},{256,384},{320,448},{384,256},{4... | collective-permute-start | bytes 294920 | tf_op jit(solution)/shard_map/ppermute | solution.py:290
  92.3 0.0 collective-permute-done.1
  92.3 1.3 %collective-permute-done.3 = bf16[4,48,256]{2,1,0:T(8,128)(2,1)S(1)} collective-permute-done((bf16[4,48,256]{2,1,0:T(8,128)(2,1)S(1)}, bf16[4,48,256]{2,1,0:T(8,128)(2,1)S(1)}, u32[]{:S(2)}, u32[]{:S(2)}) %collective-permute-start.3) | collective-permute-done | bytes 98336 | tf_op jit(solution)/shard_map/ppermute | solution.py:290
  93.6 5.6 %collective-permute-done.2 = bf16[4,48,256]{2,1,0:T(8,128)(2,1)S(1)} collective-permute-done((bf16[4,48,256]{2,1,0:T(8,128)(2,1)S(1)}, bf16[4,48,256]{2,1,0:T(8,128)(2,1)S(1)}, u32[]{:S(2)}, u32[]{:S(2)}) %collective-permute-start.2) | collective-permute-done | bytes 98336 | tf_op jit(solution)/shard_map/ppermute | solution.py:290
  99.2 0.1 fusion.7
  99.3 7.4 %collective-permute-start.4 = (bf16[48,256]{1,0:T(8,128)(2,1)S(1)}, bf16[48,256]{1,0:T(8,128)(2,1)S(1)}, u32[]{:S(2)}, u32[]{:S(2)}) collective-permute-start(bf16[48,256]{1,0:T(8,128)(2,1)S(1)} %get-tuple-element.25), channel_id=1, source_target_pairs={{0,16},{16,0},{64,80},{80,64},{128,144},{144,128},{192,208},{208,1... | collective-permute-start | bytes 73736 | tf_op jit(solution)/shard_map/ppermute | solution.py:300
  106.7 3.4 %collective-permute-start.6 = (bf16[48,256]{1,0:T(8,128)(2,1)S(1)}, bf16[48,256]{1,0:T(8,128)(2,1)S(1)}, u32[]{:S(2)}, u32[]{:S(2)}) collective-permute-start(bf16[48,256]{1,0:T(8,128)(2,1)S(1)} %get-tuple-element.26), channel_id=1, source_target_pairs={{0,272},{16,256},{64,336},{80,320},{128,400},{144,384},{192,464},{... | collective-permute-start | bytes 73736 | tf_op jit(solution)/shard_map/ppermute | solution.py:300
  110.1 6.2 %collective-permute-start.5 = (bf16[48,256]{1,0:T(8,128)(2,1)S(1)}, bf16[48,256]{1,0:T(8,128)(2,1)S(1)}, u32[]{:S(2)}, u32[]{:S(2)}) collective-permute-start(bf16[48,256]{1,0:T(8,128)(2,1)S(1)} %get-tuple-element.27), channel_id=1, source_target_pairs={{0,256},{16,272},{64,320},{80,336},{128,384},{144,400},{192,448},{... | collective-permute-start | bytes 73736 | tf_op jit(solution)/shard_map/ppermute | solution.py:300
  116.3 0.0 collective-permute-done.4
  116.3 0.0 collective-permute-done.6
  116.3 3.7 %collective-permute-done.5 = bf16[48,256]{1,0:T(8,128)(2,1)S(1)} collective-permute-done((bf16[48,256]{1,0:T(8,128)(2,1)S(1)}, bf16[48,256]{1,0:T(8,128)(2,1)S(1)}, u32[]{:S(2)}, u32[]{:S(2)}) %collective-permute-start.5) | collective-permute-done | bytes 24608 | tf_op jit(solution)/shard_map/ppermute | solution.py:300
  120.0 0.6 fusion.10
  120.7 0.0 all-to-all-done.1.text_ref
  120.7 3.5 %collect.1 = (bf16[128,4096]{1,0:T(8,128)(2,1)}, bf16[128,4096]{1,0:T(8,128)(2,1)}) custom-call(bf16[16,4,128,128]{3,2,1,0:T(8,128)(2,1)} %all-to-all-done.1.text_ref), custom_call_target="tpu_custom_call" | custom-call | bytes 4194304 | tf_op jit(solution)/shard_map/collect/pallas_call | solution.py:112
  (3 shorter events, 0.0 us)
Async XLA Ops:
  5.5 10.3 %copy-start.3 = (bf16[56,256]{1,0:T(8,128)(2,1)S(1)}, bf16[56,256]{1,0:T(8,128)(2,1)}, u32[]{:S(2)}) copy-start(bf16[56,256]{1,0:T(8,128)(2,1)} %get-tuple-element.11) | copy-start | bytes 86020
  5.6 48.1 %copy-start = (s32[512,16]{0,1:T(8,128)S(1)}, s32[512,16]{0,1:T(8,128)}, u32[]{:S(2)}) copy-start(s32[512,16]{0,1:T(8,128)} %param.13) | copy-start | bytes 98308
  5.6 48.0 %copy-start.1 = (s32[16]{0:T(128)S(1)}, s32[16]{0:T(128)}, u32[]{:S(2)}) copy-start(s32[16]{0:T(128)} %text_counts_ref.1) | copy-start | bytes 196
  5.6 48.0 %copy-start.2 = (s32[16]{0:T(128)S(1)}, s32[16]{0:T(128)}, u32[]{:S(2)}) copy-start(s32[16]{0:T(128)} %latent_counts_ref.1) | copy-start | bytes 196
  5.6 48.0 %all-to-all-start = ((bf16[16,4,128,128]{3,2,1,0:T(8,128)(2,1)}), bf16[16,4,128,128]{3,2,1,0:T(8,128)(2,1)}, u32[]{:S(2)}, u32[]{:S(2)}) async-start(bf16[16,4,128,128]{3,2,1,0:T(8,128)(2,1)} %get-tuple-element.12), calls=%async_computation | async-start | bytes 4194304 | tf_op jit(solution)/shard_map/all_to_all | solution.py:324
  72.1 48.6 %all-to-all-start.1 = ((bf16[16,4,128,128]{3,2,1,0:T(8,128)(2,1)}), bf16[16,4,128,128]{3,2,1,0:T(8,128)(2,1)}, u32[]{:S(2)}, u32[]{:S(2)}) async-start(bf16[16,4,128,128]{3,2,1,0:T(8,128)(2,1)} %get-tuple-element.13), calls=%async_computation.1 | async-start | bytes 4194304 | tf_op jit(solution)/shard_map/all_to_all | solution.py:331
  79.3 3.6 %collective-permute-start = (bf16[4,4,48,256]{3,2,1,0:T(8,128)(2,1)S(1)}, bf16[4,4,48,256]{3,2,1,0:T(8,128)(2,1)S(1)}, u32[]{:S(2)}, u32[]{:S(2)}) collective-permute-start(bf16[4,4,48,256]{3,2,1,0:T(8,128)(2,1)S(1)} %get-tuple-element.17), channel_id=1, source_target_pairs={{0,32},{32,0},{1,33},{33,1},{2,34},{34,2},{3,35},{35,3},{4,36},{36... | collective-permute-start | bytes 1179656 | tf_op jit(solution)/shard_map/ppermute | solution.py:283
  83.1 9.2 %collective-permute-start.1 = (bf16[4,48,256]{2,1,0:T(8,128)(2,1)S(1)}, bf16[4,48,256]{2,1,0:T(8,128)(2,1)S(1)}, u32[]{:S(2)}, u32[]{:S(2)}) collective-permute-start(bf16[4,48,256]{2,1,0:T(8,128)(2,1)S(1)} %get-tuple-element.22), channel_id=1, source_target_pairs={{0,64},{64,0},{128,192},{192,128},{256,320},{320,256},{384,448},{4... | collective-permute-start | bytes 294920 | tf_op jit(solution)/shard_map/ppermute | solution.py:290
  85.0 8.6 %collective-permute-start.3 = (bf16[4,48,256]{2,1,0:T(8,128)(2,1)S(1)}, bf16[4,48,256]{2,1,0:T(8,128)(2,1)S(1)}, u32[]{:S(2)}, u32[]{:S(2)}) collective-permute-start(bf16[4,48,256]{2,1,0:T(8,128)(2,1)S(1)} %get-tuple-element.23), channel_id=1, source_target_pairs={{0,192},{64,128},{128,64},{192,0},{256,448},{320,384},{384,320},{4... | collective-permute-start | bytes 294920 | tf_op jit(solution)/shard_map/ppermute | solution.py:290
  88.6 10.6 %collective-permute-start.2 = (bf16[4,48,256]{2,1,0:T(8,128)(2,1)S(1)}, bf16[4,48,256]{2,1,0:T(8,128)(2,1)S(1)}, u32[]{:S(2)}, u32[]{:S(2)}) collective-permute-start(bf16[4,48,256]{2,1,0:T(8,128)(2,1)S(1)} %get-tuple-element.24), channel_id=1, source_target_pairs={{0,128},{64,192},{128,0},{192,64},{256,384},{320,448},{384,256},{4... | collective-permute-start | bytes 294920 | tf_op jit(solution)/shard_map/ppermute | solution.py:290
  99.3 17.1 %collective-permute-start.4 = (bf16[48,256]{1,0:T(8,128)(2,1)S(1)}, bf16[48,256]{1,0:T(8,128)(2,1)S(1)}, u32[]{:S(2)}, u32[]{:S(2)}) collective-permute-start(bf16[48,256]{1,0:T(8,128)(2,1)S(1)} %get-tuple-element.25), channel_id=1, source_target_pairs={{0,16},{16,0},{64,80},{80,64},{128,144},{144,128},{192,208},{208,1... | collective-permute-start | bytes 73736 | tf_op jit(solution)/shard_map/ppermute | solution.py:300
  106.7 9.7 %collective-permute-start.6 = (bf16[48,256]{1,0:T(8,128)(2,1)S(1)}, bf16[48,256]{1,0:T(8,128)(2,1)S(1)}, u32[]{:S(2)}, u32[]{:S(2)}) collective-permute-start(bf16[48,256]{1,0:T(8,128)(2,1)S(1)} %get-tuple-element.26), channel_id=1, source_target_pairs={{0,272},{16,256},{64,336},{80,320},{128,400},{144,384},{192,464},{... | collective-permute-start | bytes 73736 | tf_op jit(solution)/shard_map/ppermute | solution.py:300
  110.1 9.9 %collective-permute-start.5 = (bf16[48,256]{1,0:T(8,128)(2,1)S(1)}, bf16[48,256]{1,0:T(8,128)(2,1)S(1)}, u32[]{:S(2)}, u32[]{:S(2)}) collective-permute-start(bf16[48,256]{1,0:T(8,128)(2,1)S(1)} %get-tuple-element.27), channel_id=1, source_target_pairs={{0,256},{16,272},{64,320},{80,336},{128,384},{144,400},{192,448},{... | collective-permute-start | bytes 73736 | tf_op jit(solution)/shard_map/ppermute | solution.py:300

commit v2 on v1

--- a/solution.py
+++ b/solution.py
@@ -13,43 +13,20 @@
 HIDDEN = -1e30
 GATE_ROWS = 8
 NEAR = 4
+SUBS = 2
+SIZES = (256, 384, 448, 512, 768)
 
 
 def spread_kernel(
-    gate_ref,
-    latent_key_ref,
-    latent_value_ref,
-    query_ref,
-    grad_ref,
-    text_ref,
-    packed_ref,
-    held_ref,
-    in_sems,
-    out_sems,
+    gate_ref, query_ref, grad_ref, latent_key_ref, latent_value_ref, text_ref, packed_ref
 ):
     peers, kinds, _, width = text_ref.shape
-    halves = kinds // 2
-    chunks = in_sems.shape[1]
-    chunk = query_ref.shape[1] // chunks
-    chunk_peers = halves * peers // chunks
-
-    def bring(kind, c):
-        columns = pl.ds(c * chunk, chunk)
-        source = (query_ref, grad_ref)[kind].at[:, columns]
-        return pltpu.make_async_copy(source, held_ref.at[kind, :, columns], in_sems.at[kind, c])
-
-    def put(kind, head):
-        half, peer = head // peers, head % peers
-        return pltpu.make_async_copy(
-            held_ref.at[kind, :, pl.ds(head * width, width)],
-            text_ref.at[peer, 2 * half + kind],
-            out_sems.at[kind, head],
-        )
-
-    for c in range(chunks):
-        for kind in range(2):
-            bring(kind, c).start()
     slots, dim = latent_key_ref.shape
+    for half in range(kinds // 2):
+        for peer in range(peers):
+            columns = pl.ds((half * peers + peer) * width, width)
+            text_ref[peer, 2 * half] = query_ref[:, columns]
+            text_ref[peer, 2 * half + 1] = grad_ref[:, columns]
     packed_ref[:slots, :dim] = latent_key_ref[...]
     packed_ref[:slots, dim:] = latent_value_ref[...]
     gate = jnp.full((GATE_ROWS, 2 * dim), gate_ref[0], jnp.float32)
@@ -59,41 +36,26 @@
     lane = lax.broadcasted_iota(jnp.int32, gate.shape, 1)
     terms = jnp.where(lane == 0, first, jnp.where(lane == 1, second, third))
     packed_ref[slots:, :] = jnp.where(lane < 3, terms, 0.0).astype(jnp.bfloat16)
-    for c in range(chunks):
-        for kind in range(2):
-            bring(kind, c).wait()
-            for head in range(c * chunk_peers, (c + 1) * chunk_peers):
-                put(kind, head).start()
-    for head in range(halves * peers):
-        for kind in range(2):
-            put(kind, head).wait()
 
 
 def spread(gate_logits, queries, cotangent, latent_keys, latent_values, halves, peers):
     rows, columns = queries.shape
     width = columns // (halves * peers)
     slots, dim = latent_keys.shape
-    chunks = 4
     vmem = pl.BlockSpec(memory_space=pltpu.VMEM)
-    anywhere = pl.BlockSpec(memory_space=pl.ANY)
     return pl.pallas_call(
         spread_kernel,
-        in_specs=[pl.BlockSpec(memory_space=pltpu.SMEM), vmem, vmem, anywhere, anywhere],
-        out_specs=[anywhere, vmem],
+        in_specs=[pl.BlockSpec(memory_space=pltpu.SMEM), vmem, vmem, vmem, vmem],
+        out_specs=[vmem, vmem],
         out_shape=[
             jax.ShapeDtypeStruct((peers, 2 * halves, rows, width), queries.dtype),
             jax.ShapeDtypeStruct((slots + GATE_ROWS, 2 * dim), queries.dtype),
-        ],
-        scratch_shapes=[
-            pltpu.VMEM((2, rows, columns), queries.dtype),
-            pltpu.SemaphoreType.DMA((2, chunks)),
-            pltpu.SemaphoreType.DMA((2, halves * peers)),
         ],
         name="spread",
         cost_estimate=pl.CostEstimate(
             flops=0, bytes_accessed=8 * rows * columns, transcendentals=0
         ),
-    )(gate_logits, latent_keys, latent_values, queries, cotangent)
+    )(gate_logits, queries, cotangent, latent_keys, latent_values)
 
 
 def collect_kernel(text_ref, mixed_ref, grad_ref):
@@ -136,6 +98,8 @@
     gate_ref,
     key_sum_ref,
     value_sum_ref,
+    hidden_ref,
+    starts_ref,
 ):
     step = pl.program_id(1)
     steps = pl.num_programs(1)
@@ -152,16 +116,27 @@
 
     @pl.when(step == 0)
     def _():
+        key_sum_ref[...] = jnp.zeros_like(key_sum_ref)
+        value_sum_ref[...] = jnp.zeros_like(value_sum_ref)
+        hidden_ref[...] = jnp.full(hidden_ref.shape, HIDDEN, jnp.float32)
+        start = 0
         for s in range(segments):
-            at = pl.ds(s * slots, slots)
+            at = pl.ds(start, slots)
             latent = latent_ref.at[s % cores, s // cores]
-            key_ref[at, :dim] = latent[:slots, :dim]
-            value_ref[at, :] = latent[:slots, dim:]
-            slot_ok = lax.broadcasted_iota(jnp.int32, (slots, lanes), 0) < latent_counts_ref[s]
+            count = jnp.where(s <= seg_index, latent_counts_ref[s], 0)
+            key_sum_ref[at, :] = latent[:slots, :dim].astype(jnp.float32)
+            value_sum_ref[at, :] = latent[:slots, dim:].astype(jnp.float32)
+            slot_ok = lax.broadcasted_iota(jnp.int32, (slots, lanes), 0) < count
             seen = jnp.broadcast_to(visible_ref[s : s + 1, :] > 0, (slots, lanes))
-            key_ref[at, dim:] = jnp.where(slot_ok & seen, 0.0, HIDDEN).astype(jnp.bfloat16)
-        key_turned_ref[...] = key_ref[:, :dim].astype(jnp.float32).T.astype(jnp.bfloat16)
-        value_turned_ref[...] = value_ref[...].astype(jnp.float32).T.astype(jnp.bfloat16)
+            hidden_ref[at, :] = jnp.where(slot_ok & seen, 0.0, HIDDEN)
+            starts_ref[s] = jnp.asarray(start, jnp.int32)
+            start = start + count
+        starts_ref[segments] = start
+        key_ref[:, :dim] = key_sum_ref[...].astype(jnp.bfloat16)
+        key_ref[:, dim:] = hidden_ref[...].astype(jnp.bfloat16)
+        value_ref[...] = value_sum_ref[...].astype(jnp.bfloat16)
+        key_turned_ref[...] = key_sum_ref[...].T.astype(jnp.bfloat16)
+        value_turned_ref[...] = value_sum_ref[...].T.astype(jnp.bfloat16)
         terms = latent_ref[0, 0, slots:, :dim].astype(jnp.float32)[0:1, :]
         gate_ref[...] = jnp.tanh(jnp.broadcast_to(jnp.sum(terms, axis=1, keepdims=True), (1, dim)))
         key_sum_ref[...] = jnp.zeros_like(key_sum_ref)
@@ -171,54 +146,85 @@
     first_block = (place_ref[0] * (steps * groups)) % lanes
     first_row = step * block_rows
     gate = gate_ref[...]
-    valid_column = (
-        lax.broadcasted_iota(jnp.int32, (block_rows, dim), 0) + first_row < own_count
-    )
-    valid_row = (
-        lax.broadcasted_iota(jnp.int32, (dim, block_rows), 1) + first_row < own_count
-    )
-    query = text_ref[:, 0].reshape(block_rows, dim)
-    grad = text_ref[:, 1].reshape(block_rows, dim)
-    grad_wide = jnp.where(valid_column, grad.astype(jnp.float32) * gate, 0.0)
-    grad_out = grad_wide.astype(jnp.bfloat16)
-    block_of = lax.broadcasted_iota(jnp.int32, (groups, rows, lanes), 0).reshape(block_rows, lanes)
-    lane_of = lax.broadcasted_iota(jnp.int32, (block_rows, lanes), 1)
-    pick = jnp.where(lane_of == block_of + (first_block + step * groups), 1.0, 0.0)
-    asked = jnp.concatenate([query, pick.astype(jnp.bfloat16)], axis=1)
     turned = (((1,), (1,)), ((), ()))
-    scores = lax.dot_general(key_ref[...], asked, turned, preferred_element_type=jnp.float32)
-    top = jnp.max(scores, axis=0, keepdims=True)
-    powers = jnp.exp2((scores - top) * to_power)
-    total = jnp.sum(powers, axis=0, keepdims=True)
-    weights = (powers * (1.0 / total)).astype(jnp.bfloat16)
-    attended = jnp.dot(value_turned_ref[...], weights, preferred_element_type=jnp.float32)
-    attended = attended.astype(jnp.bfloat16).astype(jnp.float32)
-    mixed = jnp.where(valid_row, attended * gate[:, 0:1], 0.0)
-    out_ref[:, 0] = mixed.T.astype(jnp.bfloat16).reshape(groups, rows, dim)
-    grad_turned = grad_out.astype(jnp.float32).T
-    delta = jnp.sum(grad_turned * attended, axis=0, keepdims=True)
-    grad_weights = jnp.dot(
-        value_ref[...], grad_turned.astype(jnp.bfloat16), preferred_element_type=jnp.float32
-    )
-    grad_scores = (weights.astype(jnp.float32) * (grad_weights - delta)).astype(jnp.bfloat16)
-    grad_query = (
-        jnp.dot(key_turned_ref[...], grad_scores, preferred_element_type=jnp.float32) * scaling
-    )
-    out_ref[:, 1] = grad_query.T.astype(jnp.bfloat16).reshape(groups, rows, dim)
-    key_sum_ref[...] += jnp.dot(grad_scores, query, preferred_element_type=jnp.float32)
-    value_sum_ref[...] += jnp.dot(weights, grad_out, preferred_element_type=jnp.float32)
+    sub_groups = groups // SUBS
+    sub_rows = sub_groups * rows
+    block_of = lax.broadcasted_iota(jnp.int32, (sub_groups, rows, lanes), 0)
+    block_of = block_of.reshape(sub_rows, lanes)
+    lane_of = lax.broadcasted_iota(jnp.int32, (sub_rows, lanes), 1)
+    column_of = lax.broadcasted_iota(jnp.int32, (sub_rows, dim), 0)
+    row_of = lax.broadcasted_iota(jnp.int32, (dim, sub_rows), 1)
+
+    def score(sub, size):
+        query = text_ref[sub * sub_groups : (sub + 1) * sub_groups, 0].reshape(sub_rows, dim)
+        own_block = block_of + (first_block + step * groups + sub * sub_groups)
+        pick = jnp.where(lane_of == own_block, 1.0, 0.0)
+        asked = jnp.concatenate([query, pick.astype(jnp.bfloat16)], axis=1)
+        return lax.dot_general(key_ref[:size], asked, turned, preferred_element_type=jnp.float32)
+
+    def weigh(scores):
+        top = jnp.max(scores, axis=0, keepdims=True)
+        powers = jnp.exp2((scores - top) * to_power)
+        total = jnp.sum(powers, axis=0, keepdims=True)
+        return (powers * (1.0 / total)).astype(jnp.bfloat16)
+
+    def finish(sub, size, weights):
+        at = slice(sub * sub_groups, (sub + 1) * sub_groups)
+        first = first_row + sub * sub_rows
+        query = text_ref[at, 0].reshape(sub_rows, dim)
+        grad = text_ref[at, 1].reshape(sub_rows, dim)
+        valid_column = column_of + first < own_count
+        valid_row = row_of + first < own_count
+        grad_wide = jnp.where(valid_column, grad.astype(jnp.float32) * gate, 0.0)
+        grad_out = grad_wide.astype(jnp.bfloat16)
+        attended = jnp.dot(
+            value_turned_ref[:, :size], weights, preferred_element_type=jnp.float32
+        )
+        attended = attended.astype(jnp.bfloat16).astype(jnp.float32)
+        mixed = jnp.where(valid_row, attended * gate[:, 0:1], 0.0)
+        out_ref[at, 0] = mixed.T.astype(jnp.bfloat16).reshape(sub_groups, rows, dim)
+        grad_turned = grad_out.astype(jnp.float32).T
+        delta = jnp.sum(grad_turned * attended, axis=0, keepdims=True)
+        grad_weights = jnp.dot(
+            value_ref[:size], grad_turned.astype(jnp.bfloat16), preferred_element_type=jnp.float32
+        )
+        grad_scores = weights * (grad_weights - delta).astype(jnp.bfloat16)
+        grad_query = (
+            jnp.dot(key_turned_ref[:, :size], grad_scores, preferred_element_type=jnp.float32)
+            * scaling
+        )
+        out_ref[at, 1] = grad_query.T.astype(jnp.bfloat16).reshape(sub_groups, rows, dim)
+        key_sum_ref[:size] += jnp.dot(grad_scores, query, preferred_element_type=jnp.float32)
+        value_sum_ref[:size] += jnp.dot(weights, grad_out, preferred_element_type=jnp.float32)
+
+    seen_latents = starts_ref[segments]
+    for smaller, size in zip((0,) + SIZES, SIZES):
+
+        @pl.when((seen_latents > smaller) & (seen_latents <= size))
+        def _():
+            ahead = score(0, size)
+            for sub in range(SUBS):
+                weights = weigh(ahead)
+                if sub + 1 < SUBS:
+                    ahead = score(sub + 1, size)
+                finish(sub, size, weights)
 
     @pl.when(step == steps - 1)
     def _():
         core_index = seg_index % cores
         pair_index = seg_index // cores
+        slot = lax.broadcasted_iota(jnp.int32, (slots, dim), 0)
         for near in range(NEAR):
             for far in range(pairs // NEAR):
                 pair = pair_index ^ (far * NEAR + near)
                 for ref, core in ((keep_ref, core_index), (send_ref, 1 - core_index)):
-                    at = pl.ds(pl.multiple_of((pair * cores + core) * slots, 8), slots)
-                    ref[near, far, :, :dim] = (key_sum_ref[at, :] * scaling).astype(ref.dtype)
-                    ref[near, far, :, dim:] = value_sum_ref[at, :].astype(ref.dtype)
+                    segment = pair * cores + core
+                    at = pl.ds(starts_ref[segment], slots)
+                    own = slot < starts_ref[segment + 1] - starts_ref[segment]
+                    key_part = jnp.where(own, key_sum_ref[at, :] * scaling, 0.0)
+                    value_part = jnp.where(own, value_sum_ref[at, :], 0.0)
+                    ref[near, far, :, :dim] = key_part.astype(ref.dtype)
+                    ref[near, far, :, dim:] = value_part.astype(ref.dtype)
 
 
 def attend_heads(place, text_counts, latent_counts, latents, visible_turned, text, groups):
@@ -256,6 +262,8 @@
             pltpu.VMEM((1, dim), jnp.float32),
             pltpu.VMEM((lat, dim), jnp.float32),
             pltpu.VMEM((lat, dim), jnp.float32),
+            pltpu.VMEM((lat, lanes), jnp.float32),
+            pltpu.SMEM((cores * pairs + 1,), jnp.int32),
         ],
     )
     sums = (NEAR, halves * fars, slots, 2 * dim)
@@ -326,7 +334,7 @@
     latents = lax.all_gather(latents, "core", axis=0, tiled=True)
     latents = latents.reshape(lax.axis_size("core"), halves, lax.axis_size("z_lo"), *packed.shape)
     out, keep, send = attend_heads(
-        place, text_counts, latent_counts, latents, visibility.T, text, groups=4
+        place, text_counts, latent_counts, latents, visibility.T, text, groups=8
     )
     out = lax.all_to_all(out, ("x", "y"), split_axis=0, concat_axis=0, tiled=True)
     grads = add_up(keep, send)

time: 125 us -> 117 us (0.936)
  Pallas kernels: 26.2 us -> 16.8 us
  waiting for transfers between devices: 12.3 us -> 13.9 us
    pallas_call x1, Pallas kernels: 18.4 us -> 10.1 us  [attend_heads(): pl.pallas_call(heads_kernel, grid_spec=grid_spec, out_shape=[jax.ShapeDty...]
    ppermute x3, waiting for transfers between devices: 3.69 us -> 5.28 us  [add_up(): arrived.append(lax.ppermute(send[far - 1], ('z_lo', 'z_hi'), steps))]
where the time goes in v2:
time: 117 us; the launch traced here: 116 us
  starting transfers between devices  45.6 us (39%)
  blocking collectives  37.8 us (32%)
  Pallas kernels  16.8 us (14%)
  waiting for transfers between devices  13.9 us (12%)
  between operations  1.43 us (1%)
    all_gather x1, blocking collectives, shards(): latents = lax.all_gather(packed, ('z_hi', 'z_lo'), axis=0, tiled=True)  35.4 us
    ppermute x3, starting transfers between devices, add_up(): arrived.append(lax.ppermute(send[far - 1], ('z_lo', 'z_hi'), steps))  17 us
    all_to_all x1, starting transfers between devices, shards(): lax.all_to_all(text, ('x', 'y'), split_axis=0, concat_axis=0, tiled=True)  10.2 us
    pallas_call x1, Pallas kernels, attend_heads(): pl.pallas_call(heads_kernel, grid_spec=grid_spec, out_shape=[jax.ShapeDty...  10.1 us
    ppermute x3, starting transfers between devices, add_up(): arrived.append(lax.ppermute(send[near - 1], 'z_lo', steps))  9.21 us
    all_to_all x1, starting transfers between devices, shards(): lax.all_to_all(out, ('x', 'y'), split_axis=0, concat_axis=0, tiled=True)  7.22 us
    ppermute x3, waiting for transfers between devices, add_up(): arrived.append(lax.ppermute(send[near - 1], 'z_lo', steps))  6.9 us
    ppermute x3, waiting for transfers between devices, add_up(): arrived.append(lax.ppermute(send[far - 1], ('z_lo', 'z_hi'), steps))  5.28 us
  transfers between devices with their start and end apart: 9, of which 4 were waited for; matrix products, arithmetic and copies ran while one was open for 1% of the time, Pallas kernels for 0%

profile of v2, /device:TPU:6, one launch (start us, length us, event | category | flops | bytes accessed | tf_op | source)
XLA Modules:
  0.0 116.4 jit_solution(12296341155511974505)
XLA Ops:
  1.3 3.2 %spread.1 = (bf16[16,4,128,128]{3,2,1,0:T(8,128)(2,1)}, bf16[56,256]{1,0:T(8,128)(2,1)}) custom-call(f32[1]{0:T(128)S(6)} %copy.12.gate_ref, bf16[128,4096]{1,0:T(8,128)(2,1)} %query_ref.1, bf16[128,4096]{1,0:T(8,128)(2,1)} %grad_ref.1, bf16[48,128]{1,0:T(8,128)(2,1)} %latent_key_ref.1, bf16[48,128]{1,0:T(8,128)(2,1)} %latent_value_ref.1), custom_call_target="tpu_custom_call" | custom-call | bytes 4194304 | tf_op jit(solution)/shard_map/spread/pallas_call | solution.py:46
  4.5 0.0 copy-start.3
  4.5 0.0 copy-start
  4.5 0.0 copy-start.1
  4.5 0.0 copy-start.2
  4.5 10.2 %all-to-all-start = ((bf16[16,4,128,128]{3,2,1,0:T(8,128)(2,1)}), bf16[16,4,128,128]{3,2,1,0:T(8,128)(2,1)}, u32[]{:S(2)}, u32[]{:S(2)}) async-start(bf16[16,4,128,128]{3,2,1,0:T(8,128)(2,1)} %get-tuple-element.12), calls=%async_computation | async-start | bytes 4194304 | tf_op jit(solution)/shard_map/all_to_all | solution.py:332
  14.7 0.0 copy-done.3
  14.7 35.4 %all_gather.6 = bf16[896,256]{1,0:T(8,128)(2,1)S(1)} all-gather(bf16[56,256]{1,0:T(8,128)(2,1)S(1)} %copy-done.3), channel_id=1, replica_groups=mesh['z_lo'=8,'core'=2,'z_hi'=2,'x'=4,'y'=4] {'z_hi','z_lo'}, dimensions={0}, use_global_device_ids=true | all-gather | bytes 487424 | tf_op jit(solution)/shard_map/all_gather | solution.py:333
  50.1 2.5 %all_gather.7 = bf16[1792,256]{1,0:T(8,128)(2,1)S(1)} all-gather(bf16[896,256]{1,0:T(8,128)(2,1)S(1)} %all_gather.6), channel_id=1, replica_groups=mesh['z_lo'=8,'core'=2,'z_hi'=2,'x'=4,'y'=4] {'core'}, dimensions={0}, use_global_device_ids=true | all-gather | bytes 1376256 | tf_op jit(solution)/shard_map/all_gather | solution.py:334
  52.5 0.0 all-to-all-done.text_ref
  52.5 0.0 copy-done
  52.5 0.0 copy-done.1
  52.5 0.0 copy-done.2
  52.5 10.1 %attend_heads.1 = (bf16[16,4,128,128]{3,2,1,0:T(8,128)(2,1)}, f32[4,4,48,256]{3,2,1,0:T(8,128)S(1)}, bf16[4,4,48,256]{3,2,1,0:T(8,128)(2,1)S(1)}) custom-call(s32[1]{0:T(128)} %bitcast.place_ref, s32[16]{0:T(128)S(1)} %copy-done.1, s32[16]{0:T(128)S(1)} %copy-done.2, bf16[2,2,8,56,256]{4,3,2,1,0:T(8,128)(2,1)S(1)} %bitcast.34, s32[16,512]{1,0:T(8,128)S(1)} %bitcast.35, ...), custom_call_target="tpu_custom_call" | custom-call | flops 4831838208 | bytes 4194304 | tf_op jit(solution)/shard_map/attend_heads/pallas_call | solution.py:270
  62.7 7.2 %all-to-all-start.1 = ((bf16[16,4,128,128]{3,2,1,0:T(8,128)(2,1)}), bf16[16,4,128,128]{3,2,1,0:T(8,128)(2,1)}, u32[]{:S(2)}, u32[]{:S(2)}) async-start(bf16[16,4,128,128]{3,2,1,0:T(8,128)(2,1)} %get-tuple-element.13), calls=%async_computation.1 | async-start | bytes 4194304 | tf_op jit(solution)/shard_map/all_to_all | solution.py:339
  69.9 1.9 %collective-permute-start = (bf16[4,4,48,256]{3,2,1,0:T(8,128)(2,1)S(1)}, bf16[4,4,48,256]{3,2,1,0:T(8,128)(2,1)S(1)}, u32[]{:S(2)}, u32[]{:S(2)}) collective-permute-start(bf16[4,4,48,256]{3,2,1,0:T(8,128)(2,1)S(1)} %get-tuple-element.17), channel_id=1, source_target_pairs={{0,32},{32,0},{1,33},{33,1},{2,34},{34,2},{3,35},{35,3},{4,36},{36... | collective-permute-start | bytes 1179656 | tf_op jit(solution)/shard_map/ppermute | solution.py:291
  71.8 1.7 %collective-permute-done = bf16[4,4,48,256]{3,2,1,0:T(8,128)(2,1)S(1)} collective-permute-done((bf16[4,4,48,256]{3,2,1,0:T(8,128)(2,1)S(1)}, bf16[4,4,48,256]{3,2,1,0:T(8,128)(2,1)S(1)}, u32[]{:S(2)}, u32[]{:S(2)}) %collective-permute-start) | collective-permute-done | bytes 393248 | tf_op jit(solution)/shard_map/ppermute | solution.py:291
  73.5 0.1 fusion.9
  73.7 1.9 %collective-permute-start.1 = (bf16[4,48,256]{2,1,0:T(8,128)(2,1)S(1)}, bf16[4,48,256]{2,1,0:T(8,128)(2,1)S(1)}, u32[]{:S(2)}, u32[]{:S(2)}) collective-permute-start(bf16[4,48,256]{2,1,0:T(8,128)(2,1)S(1)} %get-tuple-element.22), channel_id=1, source_target_pairs={{0,64},{64,0},{128,192},{192,128},{256,320},{320,256},{384,448},{4... | collective-permute-start | bytes 294920 | tf_op jit(solution)/shard_map/ppermute | solution.py:298
  75.6 3.6 %collective-permute-start.3 = (bf16[4,48,256]{2,1,0:T(8,128)(2,1)S(1)}, bf16[4,48,256]{2,1,0:T(8,128)(2,1)S(1)}, u32[]{:S(2)}, u32[]{:S(2)}) collective-permute-start(bf16[4,48,256]{2,1,0:T(8,128)(2,1)S(1)} %get-tuple-element.23), channel_id=1, source_target_pairs={{0,192},{64,128},{128,64},{192,0},{256,448},{320,384},{384,320},{4... | collective-permute-start | bytes 294920 | tf_op jit(solution)/shard_map/ppermute | solution.py:298
  79.2 3.7 %collective-permute-start.2 = (bf16[4,48,256]{2,1,0:T(8,128)(2,1)S(1)}, bf16[4,48,256]{2,1,0:T(8,128)(2,1)S(1)}, u32[]{:S(2)}, u32[]{:S(2)}) collective-permute-start(bf16[4,48,256]{2,1,0:T(8,128)(2,1)S(1)} %get-tuple-element.24), channel_id=1, source_target_pairs={{0,128},{64,192},{128,0},{192,64},{256,384},{320,448},{384,256},{4... | collective-permute-start | bytes 294920 | tf_op jit(solution)/shard_map/ppermute | solution.py:298
  82.9 0.0 collective-permute-done.1
  82.9 1.3 %collective-permute-done.3 = bf16[4,48,256]{2,1,0:T(8,128)(2,1)S(1)} collective-permute-done((bf16[4,48,256]{2,1,0:T(8,128)(2,1)S(1)}, bf16[4,48,256]{2,1,0:T(8,128)(2,1)S(1)}, u32[]{:S(2)}, u32[]{:S(2)}) %collective-permute-start.3) | collective-permute-done | bytes 98336 | tf_op jit(solution)/shard_map/ppermute | solution.py:298
  84.2 5.6 %collective-permute-done.2 = bf16[4,48,256]{2,1,0:T(8,128)(2,1)S(1)} collective-permute-done((bf16[4,48,256]{2,1,0:T(8,128)(2,1)S(1)}, bf16[4,48,256]{2,1,0:T(8,128)(2,1)S(1)}, u32[]{:S(2)}, u32[]{:S(2)}) %collective-permute-start.2) | collective-permute-done | bytes 98336 | tf_op jit(solution)/shard_map/ppermute | solution.py:298
  89.8 0.1 fusion.7
  89.9 7.4 %collective-permute-start.4 = (bf16[48,256]{1,0:T(8,128)(2,1)S(1)}, bf16[48,256]{1,0:T(8,128)(2,1)S(1)}, u32[]{:S(2)}, u32[]{:S(2)}) collective-permute-start(bf16[48,256]{1,0:T(8,128)(2,1)S(1)} %get-tuple-element.25), channel_id=1, source_target_pairs={{0,16},{16,0},{64,80},{80,64},{128,144},{144,128},{192,208},{208,1... | collective-permute-start | bytes 73736 | tf_op jit(solution)/shard_map/ppermute | solution.py:308
  97.3 5.0 %collective-permute-start.6 = (bf16[48,256]{1,0:T(8,128)(2,1)S(1)}, bf16[48,256]{1,0:T(8,128)(2,1)S(1)}, u32[]{:S(2)}, u32[]{:S(2)}) collective-permute-start(bf16[48,256]{1,0:T(8,128)(2,1)S(1)} %get-tuple-element.26), channel_id=1, source_target_pairs={{0,272},{16,256},{64,336},{80,320},{128,400},{144,384},{192,464},{... | collective-permute-start | bytes 73736 | tf_op jit(solution)/shard_map/ppermute | solution.py:308
  102.3 4.6 %collective-permute-start.5 = (bf16[48,256]{1,0:T(8,128)(2,1)S(1)}, bf16[48,256]{1,0:T(8,128)(2,1)S(1)}, u32[]{:S(2)}, u32[]{:S(2)}) collective-permute-start(bf16[48,256]{1,0:T(8,128)(2,1)S(1)} %get-tuple-element.27), channel_id=1, source_target_pairs={{0,256},{16,272},{64,320},{80,336},{128,384},{144,400},{192,448},{... | collective-permute-start | bytes 73736 | tf_op jit(solution)/shard_map/ppermute | solution.py:308
  106.9 0.0 collective-permute-done.4
  107.0 0.0 collective-permute-done.6
  107.0 5.3 %collective-permute-done.5 = bf16[48,256]{1,0:T(8,128)(2,1)S(1)} collective-permute-done((bf16[48,256]{1,0:T(8,128)(2,1)S(1)}, bf16[48,256]{1,0:T(8,128)(2,1)S(1)}, u32[]{:S(2)}, u32[]{:S(2)}) %collective-permute-start.5) | collective-permute-done | bytes 24608 | tf_op jit(solution)/shard_map/ppermute | solution.py:308
  112.3 0.6 fusion.10
  112.9 0.0 all-to-all-done.1.text_ref
  112.9 3.5 %collect.1 = (bf16[128,4096]{1,0:T(8,128)(2,1)}, bf16[128,4096]{1,0:T(8,128)(2,1)}) custom-call(bf16[16,4,128,128]{3,2,1,0:T(8,128)(2,1)} %all-to-all-done.1.text_ref), custom_call_target="tpu_custom_call" | custom-call | bytes 4194304 | tf_op jit(solution)/shard_map/collect/pallas_call | solution.py:74
  (3 shorter events, 0.0 us)
Async XLA Ops:
  4.5 10.2 %copy-start.3 = (bf16[56,256]{1,0:T(8,128)(2,1)S(1)}, bf16[56,256]{1,0:T(8,128)(2,1)}, u32[]{:S(2)}) copy-start(bf16[56,256]{1,0:T(8,128)(2,1)} %get-tuple-element.11) | copy-start | bytes 86020
  4.5 48.0 %copy-start = (s32[512,16]{0,1:T(8,128)S(1)}, s32[512,16]{0,1:T(8,128)}, u32[]{:S(2)}) copy-start(s32[512,16]{0,1:T(8,128)} %param.13) | copy-start | bytes 98308
  4.5 48.0 %copy-start.1 = (s32[16]{0:T(128)S(1)}, s32[16]{0:T(128)}, u32[]{:S(2)}) copy-start(s32[16]{0:T(128)} %text_counts_ref.1) | copy-start | bytes 196
  4.5 48.0 %copy-start.2 = (s32[16]{0:T(128)S(1)}, s32[16]{0:T(128)}, u32[]{:S(2)}) copy-start(s32[16]{0:T(128)} %latent_counts_ref.1) | copy-start | bytes 196
  4.5 48.0 %all-to-all-start = ((bf16[16,4,128,128]{3,2,1,0:T(8,128)(2,1)}), bf16[16,4,128,128]{3,2,1,0:T(8,128)(2,1)}, u32[]{:S(2)}, u32[]{:S(2)}) async-start(bf16[16,4,128,128]{3,2,1,0:T(8,128)(2,1)} %get-tuple-element.12), calls=%async_computation | async-start | bytes 4194304 | tf_op jit(solution)/shard_map/all_to_all | solution.py:332
  62.7 50.2 %all-to-all-start.1 = ((bf16[16,4,128,128]{3,2,1,0:T(8,128)(2,1)}), bf16[16,4,128,128]{3,2,1,0:T(8,128)(2,1)}, u32[]{:S(2)}, u32[]{:S(2)}) async-start(bf16[16,4,128,128]{3,2,1,0:T(8,128)(2,1)} %get-tuple-element.13), calls=%async_computation.1 | async-start | bytes 4194304 | tf_op jit(solution)/shard_map/all_to_all | solution.py:339
  69.9 3.6 %collective-permute-start = (bf16[4,4,48,256]{3,2,1,0:T(8,128)(2,1)S(1)}, bf16[4,4,48,256]{3,2,1,0:T(8,128)(2,1)S(1)}, u32[]{:S(2)}, u32[]{:S(2)}) collective-permute-start(bf16[4,4,48,256]{3,2,1,0:T(8,128)(2,1)S(1)} %get-tuple-element.17), channel_id=1, source_target_pairs={{0,32},{32,0},{1,33},{33,1},{2,34},{34,2},{3,35},{35,3},{4,36},{36... | collective-permute-start | bytes 1179656 | tf_op jit(solution)/shard_map/ppermute | solution.py:291
  73.7 9.2 %collective-permute-start.1 = (bf16[4,48,256]{2,1,0:T(8,128)(2,1)S(1)}, bf16[4,48,256]{2,1,0:T(8,128)(2,1)S(1)}, u32[]{:S(2)}, u32[]{:S(2)}) collective-permute-start(bf16[4,48,256]{2,1,0:T(8,128)(2,1)S(1)} %get-tuple-element.22), channel_id=1, source_target_pairs={{0,64},{64,0},{128,192},{192,128},{256,320},{320,256},{384,448},{4... | collective-permute-start | bytes 294920 | tf_op jit(solution)/shard_map/ppermute | solution.py:298
  75.6 8.6 %collective-permute-start.3 = (bf16[4,48,256]{2,1,0:T(8,128)(2,1)S(1)}, bf16[4,48,256]{2,1,0:T(8,128)(2,1)S(1)}, u32[]{:S(2)}, u32[]{:S(2)}) collective-permute-start(bf16[4,48,256]{2,1,0:T(8,128)(2,1)S(1)} %get-tuple-element.23), channel_id=1, source_target_pairs={{0,192},{64,128},{128,64},{192,0},{256,448},{320,384},{384,320},{4... | collective-permute-start | bytes 294920 | tf_op jit(solution)/shard_map/ppermute | solution.py:298
  79.2 10.6 %collective-permute-start.2 = (bf16[4,48,256]{2,1,0:T(8,128)(2,1)S(1)}, bf16[4,48,256]{2,1,0:T(8,128)(2,1)S(1)}, u32[]{:S(2)}, u32[]{:S(2)}) collective-permute-start(bf16[4,48,256]{2,1,0:T(8,128)(2,1)S(1)} %get-tuple-element.24), channel_id=1, source_target_pairs={{0,128},{64,192},{128,0},{192,64},{256,384},{320,448},{384,256},{4... | collective-permute-start | bytes 294920 | tf_op jit(solution)/shard_map/ppermute | solution.py:298
  89.9 17.1 %collective-permute-start.4 = (bf16[48,256]{1,0:T(8,128)(2,1)S(1)}, bf16[48,256]{1,0:T(8,128)(2,1)S(1)}, u32[]{:S(2)}, u32[]{:S(2)}) collective-permute-start(bf16[48,256]{1,0:T(8,128)(2,1)S(1)} %get-tuple-element.25), channel_id=1, source_target_pairs={{0,16},{16,0},{64,80},{80,64},{128,144},{144,128},{192,208},{208,1... | collective-permute-start | bytes 73736 | tf_op jit(solution)/shard_map/ppermute | solution.py:308
  97.3 9.7 %collective-permute-start.6 = (bf16[48,256]{1,0:T(8,128)(2,1)S(1)}, bf16[48,256]{1,0:T(8,128)(2,1)S(1)}, u32[]{:S(2)}, u32[]{:S(2)}) collective-permute-start(bf16[48,256]{1,0:T(8,128)(2,1)S(1)} %get-tuple-element.26), channel_id=1, source_target_pairs={{0,272},{16,256},{64,336},{80,320},{128,400},{144,384},{192,464},{... | collective-permute-start | bytes 73736 | tf_op jit(solution)/shard_map/ppermute | solution.py:308
  102.3 9.9 %collective-permute-start.5 = (bf16[48,256]{1,0:T(8,128)(2,1)S(1)}, bf16[48,256]{1,0:T(8,128)(2,1)S(1)}, u32[]{:S(2)}, u32[]{:S(2)}) collective-permute-start(bf16[48,256]{1,0:T(8,128)(2,1)S(1)} %get-tuple-element.27), channel_id=1, source_target_pairs={{0,256},{16,272},{64,320},{80,336},{128,384},{144,400},{192,448},{... | collective-permute-start | bytes 73736 | tf_op jit(solution)/shard_map/ppermute | solution.py:308

commit v3 on v2

--- a/solution.py
+++ b/solution.py
@@ -14,7 +14,7 @@
 GATE_ROWS = 8
 NEAR = 4
 SUBS = 2
-SIZES = (256, 384, 448, 512, 768)
+SIZES = (256, 384, 416, 448, 480, 512, 768)
 
 
 def spread_kernel(
@@ -29,7 +29,7 @@
             text_ref[peer, 2 * half + 1] = grad_ref[:, columns]
     packed_ref[:slots, :dim] = latent_key_ref[...]
     packed_ref[:slots, dim:] = latent_value_ref[...]
-    gate = jnp.full((GATE_ROWS, 2 * dim), gate_ref[0], jnp.float32)
+    gate = jnp.broadcast_to(gate_ref[...], (GATE_ROWS, 2 * dim))
     first = gate.astype(jnp.bfloat16).astype(jnp.float32)
     second = (gate - first).astype(jnp.bfloat16).astype(jnp.float32)
     third = gate - first - second
@@ -45,7 +45,7 @@
     vmem = pl.BlockSpec(memory_space=pltpu.VMEM)
     return pl.pallas_call(
         spread_kernel,
-        in_specs=[pl.BlockSpec(memory_space=pltpu.SMEM), vmem, vmem, vmem, vmem],
+        in_specs=[vmem] * 5,
         out_specs=[vmem, vmem],
         out_shape=[
             jax.ShapeDtypeStruct((peers, 2 * halves, rows, width), queries.dtype),
@@ -55,7 +55,7 @@
         cost_estimate=pl.CostEstimate(
             flops=0, bytes_accessed=8 * rows * columns, transcendentals=0
         ),
-    )(gate_logits, queries, cotangent, latent_keys, latent_values)
+    )(gate_logits[:, None], queries, cotangent, latent_keys, latent_values)
 
 
 def collect_kernel(text_ref, mixed_ref, grad_ref):
@@ -75,6 +75,7 @@
         collect_kernel,
         out_shape=[whole, whole],
         name="collect",
+        compiler_params=pltpu.CompilerParams(vmem_limit_bytes=12 << 20),
         cost_estimate=pl.CostEstimate(
             flops=0, bytes_accessed=8 * rows * columns, transcendentals=0
         ),
@@ -149,17 +150,17 @@
     turned = (((1,), (1,)), ((), ()))
     sub_groups = groups // SUBS
     sub_rows = sub_groups * rows
-    block_of = lax.broadcasted_iota(jnp.int32, (sub_groups, rows, lanes), 0)
-    block_of = block_of.reshape(sub_rows, lanes)
-    lane_of = lax.broadcasted_iota(jnp.int32, (sub_rows, lanes), 1)
-    column_of = lax.broadcasted_iota(jnp.int32, (sub_rows, dim), 0)
-    row_of = lax.broadcasted_iota(jnp.int32, (dim, sub_rows), 1)
+    lane_of = lax.broadcasted_iota(jnp.int32, (1, lanes), 1)
+    row_of = lax.broadcasted_iota(jnp.int32, (1, sub_rows), 1)
 
     def score(sub, size):
         query = text_ref[sub * sub_groups : (sub + 1) * sub_groups, 0].reshape(sub_rows, dim)
-        own_block = block_of + (first_block + step * groups + sub * sub_groups)
-        pick = jnp.where(lane_of == own_block, 1.0, 0.0)
-        asked = jnp.concatenate([query, pick.astype(jnp.bfloat16)], axis=1)
+        own_block = first_block + step * groups + sub * sub_groups
+        picks = []
+        for g in range(sub_groups):
+            pick = jnp.where(lane_of == own_block + g, 1.0, 0.0).astype(jnp.bfloat16)
+            picks.append(jnp.broadcast_to(pick, (rows, lanes)))
+        asked = jnp.concatenate([query, jnp.concatenate(picks, axis=0)], axis=1)
         return lax.dot_general(key_ref[:size], asked, turned, preferred_element_type=jnp.float32)
 
     def weigh(scores):
@@ -173,29 +174,26 @@
         first = first_row + sub * sub_rows
         query = text_ref[at, 0].reshape(sub_rows, dim)
         grad = text_ref[at, 1].reshape(sub_rows, dim)
-        valid_column = column_of + first < own_count
-        valid_row = row_of + first < own_count
-        grad_wide = jnp.where(valid_column, grad.astype(jnp.float32) * gate, 0.0)
-        grad_out = grad_wide.astype(jnp.bfloat16)
+        gate_of = jnp.where(row_of + first < own_count, gate[:, 0:1], 0.0)
+        grad_out = (grad.T.astype(jnp.float32) * gate_of).astype(jnp.bfloat16)
         attended = jnp.dot(
             value_turned_ref[:, :size], weights, preferred_element_type=jnp.float32
         )
         attended = attended.astype(jnp.bfloat16).astype(jnp.float32)
-        mixed = jnp.where(valid_row, attended * gate[:, 0:1], 0.0)
-        out_ref[at, 0] = mixed.T.astype(jnp.bfloat16).reshape(sub_groups, rows, dim)
-        grad_turned = grad_out.astype(jnp.float32).T
-        delta = jnp.sum(grad_turned * attended, axis=0, keepdims=True)
-        grad_weights = jnp.dot(
-            value_ref[:size], grad_turned.astype(jnp.bfloat16), preferred_element_type=jnp.float32
-        )
+        mixed = attended * gate_of
+        out_ref[at, 0] = mixed.astype(jnp.bfloat16).T.reshape(sub_groups, rows, dim)
+        delta = jnp.sum(grad_out.astype(jnp.float32) * attended, axis=0, keepdims=True)
+        grad_weights = jnp.dot(value_ref[:size], grad_out, preferred_element_type=jnp.float32)
         grad_scores = weights * (grad_weights - delta).astype(jnp.bfloat16)
         grad_query = (
             jnp.dot(key_turned_ref[:, :size], grad_scores, preferred_element_type=jnp.float32)
             * scaling
         )
-        out_ref[at, 1] = grad_query.T.astype(jnp.bfloat16).reshape(sub_groups, rows, dim)
+        out_ref[at, 1] = grad_query.astype(jnp.bfloat16).T.reshape(sub_groups, rows, dim)
         key_sum_ref[:size] += jnp.dot(grad_scores, query, preferred_element_type=jnp.float32)
-        value_sum_ref[:size] += jnp.dot(weights, grad_out, preferred_element_type=jnp.float32)
+        value_sum_ref[:size] += lax.dot_general(
+            weights, grad_out, turned, preferred_element_type=jnp.float32
+        )
 
     seen_latents = starts_ref[segments]
     for smaller, size in zip((0,) + SIZES, SIZES):
@@ -271,12 +269,12 @@
         heads_kernel,
         grid_spec=grid_spec,
         out_shape=[
-            jax.ShapeDtypeStruct(text.shape, jnp.bfloat16),
-            jax.ShapeDtypeStruct(sums, jnp.float32),
+            pltpu.HBM(text.shape, jnp.bfloat16),
+            pltpu.HBM(sums, jnp.float32),
             jax.ShapeDtypeStruct(sums, jnp.bfloat16),
         ],
         name="attend_heads",
-        compiler_params=pltpu.CompilerParams(vmem_limit_bytes=48 << 20),
+        compiler_params=pltpu.CompilerParams(vmem_limit_bytes=24 << 20),
         cost_estimate=pl.CostEstimate(
             flops=12 * halves * peers * rows * lat * dim,
             bytes_accessed=8 * halves * peers * rows * dim,

time: 117 us -> 114 us (0.974)
  Pallas kernels: 16.8 us -> 13.8 us
    pallas_call x1, Pallas kernels: 3.49 us -> 1.9 us  [collect(): pl.pallas_call(collect_kernel, out_shape=[whole, whole], name='collect',...]
    pallas_call x2, Pallas kernels: 13.4 us -> 11.9 us  [the longest x1 8.63 us: attend_heads(): pl.pallas_call(heads_kernel, grid_spec=grid_spec, out_shape=[pltpu.HBM(te...]
where the time goes in v3:
time: 114 us
  starting transfers between devices  45.2 us (40%)
  blocking collectives  38.6 us (34%)
  Pallas kernels  13.8 us (12%)
  waiting for transfers between devices  13.7 us (12%)
  between operations  1.43 us (1%)
    all_gather x1, blocking collectives, shards(): latents = lax.all_gather(packed, ('z_hi', 'z_lo'), axis=0, tiled=True)  36.2 us
    ppermute x3, starting transfers between devices, add_up(): arrived.append(lax.ppermute(send[far - 1], ('z_lo', 'z_hi'), steps))  17 us
    all_to_all x1, starting transfers between devices, shards(): lax.all_to_all(text, ('x', 'y'), split_axis=0, concat_axis=0, tiled=True)  9.55 us
    ppermute x3, starting transfers between devices, add_up(): arrived.append(lax.ppermute(send[near - 1], 'z_lo', steps))  9.21 us
    pallas_call x1, Pallas kernels, attend_heads(): pl.pallas_call(heads_kernel, grid_spec=grid_spec, out_shape=[pltpu.HBM(te...  8.63 us
    all_to_all x1, starting transfers between devices, shards(): lax.all_to_all(out, ('x', 'y'), split_axis=0, concat_axis=0, tiled=True)  7.51 us
    ppermute x3, waiting for transfers between devices, add_up(): arrived.append(lax.ppermute(send[near - 1], 'z_lo', steps))  6.9 us
    ppermute x3, waiting for transfers between devices, add_up(): arrived.append(lax.ppermute(send[far - 1], ('z_lo', 'z_hi'), steps))  5.13 us
  transfers between devices with their start and end apart: 9, of which 4 were waited for; matrix products, arithmetic and copies ran while one was open for 1% of the time, Pallas kernels for 0%

profile of v3, /device:TPU:6, one launch (start us, length us, event | category | flops | bytes accessed | tf_op | source)
XLA Modules:
  0.0 113.6 jit_solution(8487638997769391830)
XLA Ops:
  1.3 3.2 %spread.1 = (bf16[16,4,128,128]{3,2,1,0:T(8,128)(2,1)}, bf16[56,256]{1,0:T(8,128)(2,1)}) custom-call(f32[1,1]{1,0:T(1,128)} %bitcast.35.gate_ref, bf16[128,4096]{1,0:T(8,128)(2,1)} %query_ref.1, bf16[128,4096]{1,0:T(8,128)(2,1)} %grad_ref.1, bf16[48,128]{1,0:T(8,128)(2,1)} %latent_key_ref.1, bf16[48,128]{1,0:T(8,128)(2,1)} %latent_value_ref.1), custom_call_target="tpu_custom_call" | custom-call | bytes 4194304 | tf_op jit(solution)/shard_map/spread/pallas_call | solution.py:46
  4.5 0.0 copy-start.4
  4.5 0.0 copy-start
  4.5 0.0 copy-start.1
  4.5 0.0 copy-start.2
  4.5 9.5 %all-to-all-start = ((bf16[16,4,128,128]{3,2,1,0:T(8,128)(2,1)}), bf16[16,4,128,128]{3,2,1,0:T(8,128)(2,1)S(1)}, u32[]{:S(2)}, u32[]{:S(2)}) async-start(bf16[16,4,128,128]{3,2,1,0:T(8,128)(2,1)} %get-tuple-element.12), calls=%async_computation | async-start | bytes 4194304 | tf_op jit(solution)/shard_map/all_to_all | solution.py:330
  14.1 0.0 copy-done.4
  14.1 36.2 %all_gather.6 = bf16[896,256]{1,0:T(8,128)(2,1)S(1)} all-gather(bf16[56,256]{1,0:T(8,128)(2,1)S(1)} %copy-done.4), channel_id=1, replica_groups=mesh['z_lo'=8,'core'=2,'z_hi'=2,'x'=4,'y'=4] {'z_hi','z_lo'}, dimensions={0}, use_global_device_ids=true | all-gather | bytes 487424 | tf_op jit(solution)/shard_map/all_gather | solution.py:331
  50.3 2.5 %all_gather.7 = bf16[1792,256]{1,0:T(8,128)(2,1)S(1)} all-gather(bf16[896,256]{1,0:T(8,128)(2,1)S(1)} %all_gather.6), channel_id=1, replica_groups=mesh['z_lo'=8,'core'=2,'z_hi'=2,'x'=4,'y'=4] {'core'}, dimensions={0}, use_global_device_ids=true | all-gather | bytes 1376256 | tf_op jit(solution)/shard_map/all_gather | solution.py:332
  52.7 0.0 all-to-all-done.text_ref
  52.7 0.0 copy-done
  52.7 0.0 copy-done.1
  52.7 0.0 copy-done.2
  52.7 8.6 %attend_heads.1 = (bf16[16,4,128,128]{3,2,1,0:T(8,128)(2,1)}, f32[4,4,48,256]{3,2,1,0:T(8,128)}, bf16[4,4,48,256]{3,2,1,0:T(8,128)(2,1)S(1)}) custom-call(s32[1]{0:T(128)} %bitcast.place_ref, s32[16]{0:T(128)S(1)} %copy-done.1, s32[16]{0:T(128)S(1)} %copy-done.2, bf16[2,2,8,56,256]{4,3,2,1,0:T(8,128)(2,1)S(1)} %bitcast.36, s32[16,512]{1,0:T(8,128)S(1)} %bitcast.37, ...), custom_call_target="tpu_custom_call" | custom-call | flops 4831838208 | bytes 4194304 | tf_op jit(solution)/shard_map/attend_heads/pallas_call | solution.py:268
  61.4 0.0 copy-start.3
  61.4 7.5 %all-to-all-start.1 = ((bf16[16,4,128,128]{3,2,1,0:T(8,128)(2,1)}), bf16[16,4,128,128]{3,2,1,0:T(8,128)(2,1)S(1)}, u32[]{:S(2)}, u32[]{:S(2)}) async-start(bf16[16,4,128,128]{3,2,1,0:T(8,128)(2,1)} %get-tuple-element.13), calls=%async_computation.1 | async-start | bytes 4194304 | tf_op jit(solution)/shard_map/all_to_all | solution.py:337
  68.9 1.9 %collective-permute-start = (bf16[4,4,48,256]{3,2,1,0:T(8,128)(2,1)S(1)}, bf16[4,4,48,256]{3,2,1,0:T(8,128)(2,1)S(1)}, u32[]{:S(2)}, u32[]{:S(2)}) collective-permute-start(bf16[4,4,48,256]{3,2,1,0:T(8,128)(2,1)S(1)} %get-tuple-element.17), channel_id=1, source_target_pairs={{0,32},{32,0},{1,33},{33,1},{2,34},{34,2},{3,35},{35,3},{4,36},{36... | collective-permute-start | bytes 1179656 | tf_op jit(solution)/shard_map/ppermute | solution.py:289
  70.8 1.7 %collective-permute-done = bf16[4,4,48,256]{3,2,1,0:T(8,128)(2,1)S(1)} collective-permute-done((bf16[4,4,48,256]{3,2,1,0:T(8,128)(2,1)S(1)}, bf16[4,4,48,256]{3,2,1,0:T(8,128)(2,1)S(1)}, u32[]{:S(2)}, u32[]{:S(2)}) %collective-permute-start) | collective-permute-done | bytes 393248 | tf_op jit(solution)/shard_map/ppermute | solution.py:289
  72.5 0.0 copy-done.3
  72.5 0.1 fusion.9
  72.6 1.9 %collective-permute-start.1 = (bf16[4,48,256]{2,1,0:T(8,128)(2,1)S(1)}, bf16[4,48,256]{2,1,0:T(8,128)(2,1)S(1)}, u32[]{:S(2)}, u32[]{:S(2)}) collective-permute-start(bf16[4,48,256]{2,1,0:T(8,128)(2,1)S(1)} %get-tuple-element.22), channel_id=1, source_target_pairs={{0,64},{64,0},{128,192},{192,128},{256,320},{320,256},{384,448},{4... | collective-permute-start | bytes 294920 | tf_op jit(solution)/shard_map/ppermute | solution.py:296
  74.6 3.6 %collective-permute-start.3 = (bf16[4,48,256]{2,1,0:T(8,128)(2,1)S(1)}, bf16[4,48,256]{2,1,0:T(8,128)(2,1)S(1)}, u32[]{:S(2)}, u32[]{:S(2)}) collective-permute-start(bf16[4,48,256]{2,1,0:T(8,128)(2,1)S(1)} %get-tuple-element.23), channel_id=1, source_target_pairs={{0,192},{64,128},{128,64},{192,0},{256,448},{320,384},{384,320},{4... | collective-permute-start | bytes 294920 | tf_op jit(solution)/shard_map/ppermute | solution.py:296
  78.2 3.7 %collective-permute-start.2 = (bf16[4,48,256]{2,1,0:T(8,128)(2,1)S(1)}, bf16[4,48,256]{2,1,0:T(8,128)(2,1)S(1)}, u32[]{:S(2)}, u32[]{:S(2)}) collective-permute-start(bf16[4,48,256]{2,1,0:T(8,128)(2,1)S(1)} %get-tuple-element.24), channel_id=1, source_target_pairs={{0,128},{64,192},{128,0},{192,64},{256,384},{320,448},{384,256},{4... | collective-permute-start | bytes 294920 | tf_op jit(solution)/shard_map/ppermute | solution.py:296
  81.9 0.0 collective-permute-done.1
  81.9 1.3 %collective-permute-done.3 = bf16[4,48,256]{2,1,0:T(8,128)(2,1)S(1)} collective-permute-done((bf16[4,48,256]{2,1,0:T(8,128)(2,1)S(1)}, bf16[4,48,256]{2,1,0:T(8,128)(2,1)S(1)}, u32[]{:S(2)}, u32[]{:S(2)}) %collective-permute-start.3) | collective-permute-done | bytes 98336 | tf_op jit(solution)/shard_map/ppermute | solution.py:296
  83.2 5.6 %collective-permute-done.2 = bf16[4,48,256]{2,1,0:T(8,128)(2,1)S(1)} collective-permute-done((bf16[4,48,256]{2,1,0:T(8,128)(2,1)S(1)}, bf16[4,48,256]{2,1,0:T(8,128)(2,1)S(1)}, u32[]{:S(2)}, u32[]{:S(2)}) %collective-permute-start.2) | collective-permute-done | bytes 98336 | tf_op jit(solution)/shard_map/ppermute | solution.py:296
  88.8 0.1 fusion.7
  88.9 6.9 %collective-permute-start.4 = (bf16[48,256]{1,0:T(8,128)(2,1)S(1)}, bf16[48,256]{1,0:T(8,128)(2,1)S(1)}, u32[]{:S(2)}, u32[]{:S(2)}) collective-permute-start(bf16[48,256]{1,0:T(8,128)(2,1)S(1)} %get-tuple-element.25), channel_id=1, source_target_pairs={{0,16},{16,0},{64,80},{80,64},{128,144},{144,128},{192,208},{208,1... | collective-permute-start | bytes 73736 | tf_op jit(solution)/shard_map/ppermute | solution.py:306
  95.8 5.3 %collective-permute-start.6 = (bf16[48,256]{1,0:T(8,128)(2,1)S(1)}, bf16[48,256]{1,0:T(8,128)(2,1)S(1)}, u32[]{:S(2)}, u32[]{:S(2)}) collective-permute-start(bf16[48,256]{1,0:T(8,128)(2,1)S(1)} %get-tuple-element.26), channel_id=1, source_target_pairs={{0,272},{16,256},{64,336},{80,320},{128,400},{144,384},{192,464},{... | collective-permute-start | bytes 73736 | tf_op jit(solution)/shard_map/ppermute | solution.py:306
  101.1 4.8 %collective-permute-start.5 = (bf16[48,256]{1,0:T(8,128)(2,1)S(1)}, bf16[48,256]{1,0:T(8,128)(2,1)S(1)}, u32[]{:S(2)}, u32[]{:S(2)}) collective-permute-start(bf16[48,256]{1,0:T(8,128)(2,1)S(1)} %get-tuple-element.27), channel_id=1, source_target_pairs={{0,256},{16,272},{64,320},{80,336},{128,384},{144,400},{192,448},{... | collective-permute-start | bytes 73736 | tf_op jit(solution)/shard_map/ppermute | solution.py:306
  105.9 0.0 collective-permute-done.4
  105.9 0.0 collective-permute-done.6
  105.9 5.1 %collective-permute-done.5 = bf16[48,256]{1,0:T(8,128)(2,1)S(1)} collective-permute-done((bf16[48,256]{1,0:T(8,128)(2,1)S(1)}, bf16[48,256]{1,0:T(8,128)(2,1)S(1)}, u32[]{:S(2)}, u32[]{:S(2)}) %collective-permute-start.5) | collective-permute-done | bytes 24608 | tf_op jit(solution)/shard_map/ppermute | solution.py:306
  111.1 0.6 fusion.10
  111.7 0.0 all-to-all-done.1.text_ref
  111.7 1.9 %collect.1 = (bf16[128,4096]{1,0:T(8,128)(2,1)}, bf16[128,4096]{1,0:T(8,128)(2,1)}) custom-call(bf16[16,4,128,128]{3,2,1,0:T(8,128)(2,1)S(1)} %all-to-all-done.1.text_ref), custom_call_target="tpu_custom_call" | custom-call | bytes 4194304 | tf_op jit(solution)/shard_map/collect/pallas_call | solution.py:74
  (3 shorter events, 0.0 us)
Async XLA Ops:
  4.5 9.6 %copy-start.4 = (bf16[56,256]{1,0:T(8,128)(2,1)S(1)}, bf16[56,256]{1,0:T(8,128)(2,1)}, u32[]{:S(2)}) copy-start(bf16[56,256]{1,0:T(8,128)(2,1)} %get-tuple-element.11) | copy-start | bytes 86020
  4.5 48.2 %copy-start = (s32[512,16]{0,1:T(8,128)S(1)}, s32[512,16]{0,1:T(8,128)}, u32[]{:S(2)}) copy-start(s32[512,16]{0,1:T(8,128)} %param.13) | copy-start | bytes 98308
  4.5 48.2 %copy-start.1 = (s32[16]{0:T(128)S(1)}, s32[16]{0:T(128)}, u32[]{:S(2)}) copy-start(s32[16]{0:T(128)} %text_counts_ref.1) | copy-start | bytes 196
  4.5 48.2 %copy-start.2 = (s32[16]{0:T(128)S(1)}, s32[16]{0:T(128)}, u32[]{:S(2)}) copy-start(s32[16]{0:T(128)} %latent_counts_ref.1) | copy-start | bytes 196
  4.5 48.2 %all-to-all-start = ((bf16[16,4,128,128]{3,2,1,0:T(8,128)(2,1)}), bf16[16,4,128,128]{3,2,1,0:T(8,128)(2,1)S(1)}, u32[]{:S(2)}, u32[]{:S(2)}) async-start(bf16[16,4,128,128]{3,2,1,0:T(8,128)(2,1)} %get-tuple-element.12), calls=%async_computation | async-start | bytes 4194304 | tf_op jit(solution)/shard_map/all_to_all | solution.py:330
  61.4 11.1 %copy-start.3 = (f32[4,4,48,256]{3,2,1,0:T(8,128)S(1)}, f32[4,4,48,256]{3,2,1,0:T(8,128)}, u32[]{:S(2)}) copy-start(f32[4,4,48,256]{3,2,1,0:T(8,128)} %get-tuple-element.16) | copy-start | bytes 2359300
  61.4 50.3 %all-to-all-start.1 = ((bf16[16,4,128,128]{3,2,1,0:T(8,128)(2,1)}), bf16[16,4,128,128]{3,2,1,0:T(8,128)(2,1)S(1)}, u32[]{:S(2)}, u32[]{:S(2)}) async-start(bf16[16,4,128,128]{3,2,1,0:T(8,128)(2,1)} %get-tuple-element.13), calls=%async_computation.1 | async-start | bytes 4194304 | tf_op jit(solution)/shard_map/all_to_all | solution.py:337
  68.9 3.6 %collective-permute-start = (bf16[4,4,48,256]{3,2,1,0:T(8,128)(2,1)S(1)}, bf16[4,4,48,256]{3,2,1,0:T(8,128)(2,1)S(1)}, u32[]{:S(2)}, u32[]{:S(2)}) collective-permute-start(bf16[4,4,48,256]{3,2,1,0:T(8,128)(2,1)S(1)} %get-tuple-element.17), channel_id=1, source_target_pairs={{0,32},{32,0},{1,33},{33,1},{2,34},{34,2},{3,35},{35,3},{4,36},{36... | collective-permute-start | bytes 1179656 | tf_op jit(solution)/shard_map/ppermute | solution.py:289
  72.6 9.2 %collective-permute-start.1 = (bf16[4,48,256]{2,1,0:T(8,128)(2,1)S(1)}, bf16[4,48,256]{2,1,0:T(8,128)(2,1)S(1)}, u32[]{:S(2)}, u32[]{:S(2)}) collective-permute-start(bf16[4,48,256]{2,1,0:T(8,128)(2,1)S(1)} %get-tuple-element.22), channel_id=1, source_target_pairs={{0,64},{64,0},{128,192},{192,128},{256,320},{320,256},{384,448},{4... | collective-permute-start | bytes 294920 | tf_op jit(solution)/shard_map/ppermute | solution.py:296
  74.6 8.6 %collective-permute-start.3 = (bf16[4,48,256]{2,1,0:T(8,128)(2,1)S(1)}, bf16[4,48,256]{2,1,0:T(8,128)(2,1)S(1)}, u32[]{:S(2)}, u32[]{:S(2)}) collective-permute-start(bf16[4,48,256]{2,1,0:T(8,128)(2,1)S(1)} %get-tuple-element.23), channel_id=1, source_target_pairs={{0,192},{64,128},{128,64},{192,0},{256,448},{320,384},{384,320},{4... | collective-permute-start | bytes 294920 | tf_op jit(solution)/shard_map/ppermute | solution.py:296
  78.2 10.6 %collective-permute-start.2 = (bf16[4,48,256]{2,1,0:T(8,128)(2,1)S(1)}, bf16[4,48,256]{2,1,0:T(8,128)(2,1)S(1)}, u32[]{:S(2)}, u32[]{:S(2)}) collective-permute-start(bf16[4,48,256]{2,1,0:T(8,128)(2,1)S(1)} %get-tuple-element.24), channel_id=1, source_target_pairs={{0,128},{64,192},{128,0},{192,64},{256,384},{320,448},{384,256},{4... | collective-permute-start | bytes 294920 | tf_op jit(solution)/shard_map/ppermute | solution.py:296
  88.9 17.1 %collective-permute-start.4 = (bf16[48,256]{1,0:T(8,128)(2,1)S(1)}, bf16[48,256]{1,0:T(8,128)(2,1)S(1)}, u32[]{:S(2)}, u32[]{:S(2)}) collective-permute-start(bf16[48,256]{1,0:T(8,128)(2,1)S(1)} %get-tuple-element.25), channel_id=1, source_target_pairs={{0,16},{16,0},{64,80},{80,64},{128,144},{144,128},{192,208},{208,1... | collective-permute-start | bytes 73736 | tf_op jit(solution)/shard_map/ppermute | solution.py:306
  95.8 10.1 %collective-permute-start.6 = (bf16[48,256]{1,0:T(8,128)(2,1)S(1)}, bf16[48,256]{1,0:T(8,128)(2,1)S(1)}, u32[]{:S(2)}, u32[]{:S(2)}) collective-permute-start(bf16[48,256]{1,0:T(8,128)(2,1)S(1)} %get-tuple-element.26), channel_id=1, source_target_pairs={{0,272},{16,256},{64,336},{80,320},{128,400},{144,384},{192,464},{... | collective-permute-start | bytes 73736 | tf_op jit(solution)/shard_map/ppermute | solution.py:306
  101.1 9.9 %collective-permute-start.5 = (bf16[48,256]{1,0:T(8,128)(2,1)S(1)}, bf16[48,256]{1,0:T(8,128)(2,1)S(1)}, u32[]{:S(2)}, u32[]{:S(2)}) collective-permute-start(bf16[48,256]{1,0:T(8,128)(2,1)S(1)} %get-tuple-element.27), channel_id=1, source_target_pairs={{0,256},{16,272},{64,320},{80,336},{128,384},{144,400},{192,448},{... | collective-permute-start | bytes 73736 | tf_op jit(solution)/shard_map/ppermute | solution.py:306

commit v4 on v3

--- a/solution.py
+++ b/solution.py
@@ -211,18 +211,21 @@
     def _():
         core_index = seg_index % cores
         pair_index = seg_index // cores
+        fars = pairs // NEAR
         slot = lax.broadcasted_iota(jnp.int32, (slots, dim), 0)
         for near in range(NEAR):
-            for far in range(pairs // NEAR):
-                pair = pair_index ^ (far * NEAR + near)
+            for block in range(fars):
+                pair = block * NEAR + ((pair_index % NEAR) ^ near)
+                shift = (pl.program_id(0) - half_index) * fars + block - pair_index // NEAR
+                shift = (shift + keep_ref.shape[1]) % keep_ref.shape[1]
                 for ref, core in ((keep_ref, core_index), (send_ref, 1 - core_index)):
                     segment = pair * cores + core
                     at = pl.ds(starts_ref[segment], slots)
                     own = slot < starts_ref[segment + 1] - starts_ref[segment]
                     key_part = jnp.where(own, key_sum_ref[at, :] * scaling, 0.0)
                     value_part = jnp.where(own, value_sum_ref[at, :], 0.0)
-                    ref[near, far, :, :dim] = key_part.astype(ref.dtype)
-                    ref[near, far, :, dim:] = value_part.astype(ref.dtype)
+                    ref[near, shift, :, :dim] = key_part.astype(ref.dtype)
+                    ref[near, shift, :, dim:] = value_part.astype(ref.dtype)
 
 
 def attend_heads(place, text_counts, latent_counts, latents, visible_turned, text, groups):
@@ -235,9 +238,7 @@
     steps = peers // groups
     fars = pairs // NEAR
     text_spec = pl.BlockSpec((groups, 2, rows, dim), lambda h, i, *s: (i, h, 0, 0))
-    sum_spec = pl.BlockSpec(
-        (NEAR, fars, slots, 2 * dim), lambda h, i, p, *s: (0, h ^ (p[0] % 2), 0, 0)
-    )
+    sum_spec = pl.BlockSpec((NEAR, halves * fars, slots, 2 * dim), lambda h, i, *s: (0, 0, 0, 0))
     grid_spec = pltpu.PrefetchScalarGridSpec(
         num_scalar_prefetch=3,
         grid=(halves, steps),
@@ -270,7 +271,7 @@
         grid_spec=grid_spec,
         out_shape=[
             pltpu.HBM(text.shape, jnp.bfloat16),
-            pltpu.HBM(sums, jnp.float32),
+            jax.ShapeDtypeStruct(sums, jnp.bfloat16),
             jax.ShapeDtypeStruct(sums, jnp.bfloat16),
         ],
         name="attend_heads",
@@ -284,10 +285,9 @@
 
 
 def add_up(keep, send):
-    fars = keep.shape[1] // 2
     pairs = lax.axis_size("z_lo")
     other = lax.ppermute(send, "core", [(0, 1), (1, 0)])
-    keep = keep + other.astype(jnp.float32)
+    keep = keep.astype(jnp.float32) + other.astype(jnp.float32)
     send = keep[1:].astype(jnp.bfloat16)
     keep = keep[0]
     arrived = []
@@ -296,18 +296,17 @@
         arrived.append(lax.ppermute(send[near - 1], "z_lo", steps))
     for other in arrived:
         keep = keep + other.astype(jnp.float32)
-    send = keep[1:].astype(jnp.bfloat16)
-    arrived = []
-    for far in (2, 1, 3):
-        half, block = far // fars, far % fars
-        steps = [
-            (2 * i + h, 2 * (i ^ (block * NEAR)) + (h ^ half)) for i in range(pairs) for h in range(2)
-        ]
-        arrived.append(lax.ppermute(send[far - 1], ("z_lo", "z_hi"), steps))
-    keep = keep[0]
-    for other in arrived:
-        keep = keep + other.astype(jnp.float32)
-    return keep.astype(jnp.bfloat16)
+    chips = pairs * lax.axis_size("z_hi")
+
+    def shift(piece, by):
+        flat = lambda z: z % pairs * 2 + z // pairs
+        steps = [(flat(z), flat((z + by) % chips)) for z in range(chips)]
+        return lax.ppermute(piece.astype(jnp.bfloat16), ("z_lo", "z_hi"), steps)
+
+    passing = shift(keep[2], NEAR)
+    left = shift(keep[3], -NEAR)
+    right = shift(keep[1] + passing.astype(jnp.float32), NEAR)
+    return (keep[0] + left.astype(jnp.float32) + right.astype(jnp.float32)).astype(jnp.bfloat16)
 
 
 def shards(

time: 114 us -> 110 us (0.965)
  starting transfers between devices: 45.2 us -> 42.9 us
  waiting for transfers between devices: 13.7 us -> 11.6 us
    ppermute x3, starting transfers between devices: 17 us -> 14.8 us  [shift(): return lax.ppermute(piece.astype(jnp.bfloat16), ('z_lo', 'z_hi'), steps)]
    ppermute x1, waiting for transfers between devices: 1.69 us -> 0.01 us  [add_up(): other = lax.ppermute(send, 'core', [(0, 1), (1, 0)])]
where the time goes in v4:
time: 110 us; the launch traced here: 109 us
  starting transfers between devices  42.9 us (39%)
  blocking collectives  38.6 us (35%)
  Pallas kernels  13.7 us (12%)
  waiting for transfers between devices  11.6 us (11%)
  between operations  1.42 us (1%)
    all_gather x1, blocking collectives, shards(): latents = lax.all_gather(packed, ('z_hi', 'z_lo'), axis=0, tiled=True)  36.2 us
    ppermute x3, starting transfers between devices, shift(): return lax.ppermute(piece.astype(jnp.bfloat16), ('z_lo', 'z_hi'), steps)  14.8 us
    all_to_all x1, starting transfers between devices, shards(): lax.all_to_all(text, ('x', 'y'), split_axis=0, concat_axis=0, tiled=True)  9.55 us
    ppermute x3, starting transfers between devices, add_up(): arrived.append(lax.ppermute(send[near - 1], 'z_lo', steps))  9.21 us
    pallas_call x1, Pallas kernels, attend_heads(): pl.pallas_call(heads_kernel, grid_spec=grid_spec, out_shape=[pltpu.HBM(te...  8.54 us
    all_to_all x1, starting transfers between devices, shards(): lax.all_to_all(out, ('x', 'y'), split_axis=0, concat_axis=0, tiled=True)  7.39 us
    ppermute x3, waiting for transfers between devices, add_up(): arrived.append(lax.ppermute(send[near - 1], 'z_lo', steps))  6.59 us
    ppermute x3, waiting for transfers between devices, shift(): return lax.ppermute(piece.astype(jnp.bfloat16), ('z_lo', 'z_hi'), steps)  4.96 us
  transfers between devices with their start and end apart: 9, of which 4 were waited for; matrix products, arithmetic and copies ran while one was open for 1% of the time, Pallas kernels for 0%

profile of v4, /device:TPU:6, one launch (start us, length us, event | category | flops | bytes accessed | tf_op | source)
XLA Modules:
  0.0 109.1 jit_solution(16976117115730185797)
XLA Ops:
  1.3 3.2 %spread.1 = (bf16[16,4,128,128]{3,2,1,0:T(8,128)(2,1)}, bf16[56,256]{1,0:T(8,128)(2,1)}) custom-call(f32[1,1]{1,0:T(1,128)} %bitcast.37.gate_ref, bf16[128,4096]{1,0:T(8,128)(2,1)} %query_ref.1, bf16[128,4096]{1,0:T(8,128)(2,1)} %grad_ref.1, bf16[48,128]{1,0:T(8,128)(2,1)} %latent_key_ref.1, bf16[48,128]{1,0:T(8,128)(2,1)} %latent_value_ref.1), custom_call_target="tpu_custom_call" | custom-call | bytes 4194304 | tf_op jit(solution)/shard_map/spread/pallas_call | solution.py:46
  4.5 0.0 copy-start.3
  4.5 0.0 copy-start
  4.5 0.0 copy-start.1
  4.5 0.0 copy-start.2
  4.5 9.5 %all-to-all-start = ((bf16[16,4,128,128]{3,2,1,0:T(8,128)(2,1)}), bf16[16,4,128,128]{3,2,1,0:T(8,128)(2,1)S(1)}, u32[]{:S(2)}, u32[]{:S(2)}) async-start(bf16[16,4,128,128]{3,2,1,0:T(8,128)(2,1)} %get-tuple-element.12), calls=%async_computation | async-start | bytes 4194304 | tf_op jit(solution)/shard_map/all_to_all | solution.py:329
  14.1 0.0 copy-done.3
  14.1 36.2 %all_gather.6 = bf16[896,256]{1,0:T(8,128)(2,1)S(1)} all-gather(bf16[56,256]{1,0:T(8,128)(2,1)S(1)} %copy-done.3), channel_id=1, replica_groups=mesh['z_lo'=8,'core'=2,'z_hi'=2,'x'=4,'y'=4] {'z_hi','z_lo'}, dimensions={0}, use_global_device_ids=true | all-gather | bytes 487424 | tf_op jit(solution)/shard_map/all_gather | solution.py:330
  50.3 2.5 %all_gather.7 = bf16[1792,256]{1,0:T(8,128)(2,1)S(1)} all-gather(bf16[896,256]{1,0:T(8,128)(2,1)S(1)} %all_gather.6), channel_id=1, replica_groups=mesh['z_lo'=8,'core'=2,'z_hi'=2,'x'=4,'y'=4] {'core'}, dimensions={0}, use_global_device_ids=true | all-gather | bytes 1376256 | tf_op jit(solution)/shard_map/all_gather | solution.py:331
  52.7 0.0 all-to-all-done.text_ref
  52.7 0.0 copy-done
  52.7 0.0 copy-done.1
  52.7 0.0 copy-done.2
  52.7 8.5 %attend_heads.1 = (bf16[16,4,128,128]{3,2,1,0:T(8,128)(2,1)}, bf16[4,4,48,256]{3,2,1,0:T(8,128)(2,1)S(1)}, bf16[4,4,48,256]{3,2,1,0:T(8,128)(2,1)}) custom-call(s32[1]{0:T(128)} %bitcast.place_ref, s32[16]{0:T(128)S(1)} %copy-done.1, s32[16]{0:T(128)S(1)} %copy-done.2, bf16[2,2,8,56,256]{4,3,2,1,0:T(8,128)(2,1)S(1)} %bitcast.38, s32[16,512]{1,0:T(8,128)S(1)} %bitcast.39, ...), custom_call_target="tpu_custom_call" | custom-call | flops 4831838208 | bytes 4194304 | tf_op jit(solution)/shard_map/attend_heads/pallas_call | solution.py:269
  61.3 2.0 %collective-permute-start = (bf16[4,4,48,256]{3,2,1,0:T(8,128)(2,1)}, bf16[4,4,48,256]{3,2,1,0:T(8,128)(2,1)S(1)}, u32[]{:S(2)}, u32[]{:S(2)}) collective-permute-start(bf16[4,4,48,256]{3,2,1,0:T(8,128)(2,1)} %get-tuple-element.17), channel_id=1, source_target_pairs={{0,32},{32,0},{1,33},{33,1},{2,34},{34,2},{3,35},{35,3},{4,36},{36... | collective-permute-start | bytes 1179656 | tf_op jit(solution)/shard_map/ppermute | solution.py:289
  63.3 7.4 %all-to-all-start.1 = ((bf16[16,4,128,128]{3,2,1,0:T(8,128)(2,1)}), bf16[16,4,128,128]{3,2,1,0:T(8,128)(2,1)S(1)}, u32[]{:S(2)}, u32[]{:S(2)}) async-start(bf16[16,4,128,128]{3,2,1,0:T(8,128)(2,1)} %get-tuple-element.13), calls=%async_computation.1 | async-start | bytes 4194304 | tf_op jit(solution)/shard_map/all_to_all | solution.py:336
  70.7 0.0 collective-permute-done
  70.7 0.1 convert_add_fusion
  70.9 1.9 %collective-permute-start.1 = (bf16[4,48,256]{2,1,0:T(8,128)(2,1)S(1)}, bf16[4,48,256]{2,1,0:T(8,128)(2,1)S(1)}, u32[]{:S(2)}, u32[]{:S(2)}) collective-permute-start(bf16[4,48,256]{2,1,0:T(8,128)(2,1)S(1)} %get-tuple-element.22), channel_id=1, source_target_pairs={{0,64},{64,0},{128,192},{192,128},{256,320},{320,256},{384,448},{4... | collective-permute-start | bytes 294920 | tf_op jit(solution)/shard_map/ppermute | solution.py:296
  72.8 3.6 %collective-permute-start.3 = (bf16[4,48,256]{2,1,0:T(8,128)(2,1)S(1)}, bf16[4,48,256]{2,1,0:T(8,128)(2,1)S(1)}, u32[]{:S(2)}, u32[]{:S(2)}) collective-permute-start(bf16[4,48,256]{2,1,0:T(8,128)(2,1)S(1)} %get-tuple-element.23), channel_id=1, source_target_pairs={{0,192},{64,128},{128,64},{192,0},{256,448},{320,384},{384,320},{4... | collective-permute-start | bytes 294920 | tf_op jit(solution)/shard_map/ppermute | solution.py:296
  76.4 3.7 %collective-permute-start.2 = (bf16[4,48,256]{2,1,0:T(8,128)(2,1)S(1)}, bf16[4,48,256]{2,1,0:T(8,128)(2,1)S(1)}, u32[]{:S(2)}, u32[]{:S(2)}) collective-permute-start(bf16[4,48,256]{2,1,0:T(8,128)(2,1)S(1)} %get-tuple-element.24), channel_id=1, source_target_pairs={{0,128},{64,192},{128,0},{192,64},{256,384},{320,448},{384,256},{4... | collective-permute-start | bytes 294920 | tf_op jit(solution)/shard_map/ppermute | solution.py:296
  80.1 0.0 collective-permute-done.1
  80.1 1.0 collective-permute-done.3
  81.1 5.6 %collective-permute-done.2 = bf16[4,48,256]{2,1,0:T(8,128)(2,1)S(1)} collective-permute-done((bf16[4,48,256]{2,1,0:T(8,128)(2,1)S(1)}, bf16[4,48,256]{2,1,0:T(8,128)(2,1)S(1)}, u32[]{:S(2)}, u32[]{:S(2)}) %collective-permute-start.2) | collective-permute-done | bytes 98336 | tf_op jit(solution)/shard_map/ppermute | solution.py:296
  86.7 0.1 fusion.9
  86.8 5.2 %collective-permute-start.5 = (bf16[48,256]{1,0:T(8,128)(2,1)S(1)}, bf16[48,256]{1,0:T(8,128)(2,1)S(1)}, u32[]{:S(2)}, u32[]{:S(2)}) collective-permute-start(bf16[48,256]{1,0:T(8,128)(2,1)S(1)} %get-tuple-element.26), channel_id=1, source_target_pairs={{0,256},{64,320},{128,384},{192,448},{256,16},{320,80},{384,144},{... | collective-permute-start | bytes 73736 | tf_op jit(solution)/shard_map/ppermute | solution.py:304
  91.9 4.6 %collective-permute-start.4 = (bf16[48,256]{1,0:T(8,128)(2,1)S(1)}, bf16[48,256]{1,0:T(8,128)(2,1)S(1)}, u32[]{:S(2)}, u32[]{:S(2)}) collective-permute-start(bf16[48,256]{1,0:T(8,128)(2,1)S(1)} %get-tuple-element.25), channel_id=1, source_target_pairs={{0,272},{64,336},{128,400},{192,464},{256,0},{320,64},{384,128},{4... | collective-permute-start | bytes 73736 | tf_op jit(solution)/shard_map/ppermute | solution.py:304
  96.5 0.4 collective-permute-done.5
  96.9 5.0 %collective-permute-start.6 = (bf16[48,256]{1,0:T(8,128)(2,1)S(1)}, bf16[48,256]{1,0:T(8,128)(2,1)S(1)}, u32[]{:S(2)}, u32[]{:S(2)}) collective-permute-start(bf16[48,256]{1,0:T(8,128)(2,1)S(1)} %fusion.4), channel_id=1, source_target_pairs={{0,256},{64,320},{128,384},{192,448},{256,16},{320,80},{384,144},{... | collective-permute-start | bytes 73736 | tf_op jit(solution)/shard_map/ppermute | solution.py:304
  101.9 0.0 collective-permute-done.4
  102.0 4.6 %collective-permute-done.6 = bf16[48,256]{1,0:T(8,128)(2,1)S(1)} collective-permute-done((bf16[48,256]{1,0:T(8,128)(2,1)S(1)}, bf16[48,256]{1,0:T(8,128)(2,1)S(1)}, u32[]{:S(2)}, u32[]{:S(2)}) %collective-permute-start.6) | collective-permute-done | bytes 24608 | tf_op jit(solution)/shard_map/ppermute | solution.py:304
  106.6 0.6 fusion.11
  107.2 0.0 all-to-all-done.1.text_ref
  107.2 1.9 %collect.1 = (bf16[128,4096]{1,0:T(8,128)(2,1)}, bf16[128,4096]{1,0:T(8,128)(2,1)}) custom-call(bf16[16,4,128,128]{3,2,1,0:T(8,128)(2,1)S(1)} %all-to-all-done.1.text_ref), custom_call_target="tpu_custom_call" | custom-call | bytes 4194304 | tf_op jit(solution)/shard_map/collect/pallas_call | solution.py:74
  (4 shorter events, 0.0 us)
Async XLA Ops:
  4.5 9.6 %copy-start.3 = (bf16[56,256]{1,0:T(8,128)(2,1)S(1)}, bf16[56,256]{1,0:T(8,128)(2,1)}, u32[]{:S(2)}) copy-start(bf16[56,256]{1,0:T(8,128)(2,1)} %get-tuple-element.11) | copy-start | bytes 86020
  4.5 48.2 %copy-start = (s32[512,16]{0,1:T(8,128)S(1)}, s32[512,16]{0,1:T(8,128)}, u32[]{:S(2)}) copy-start(s32[512,16]{0,1:T(8,128)} %param.13) | copy-start | bytes 98308
  4.5 48.2 %copy-start.1 = (s32[16]{0:T(128)S(1)}, s32[16]{0:T(128)}, u32[]{:S(2)}) copy-start(s32[16]{0:T(128)} %text_counts_ref.1) | copy-start | bytes 196
  4.5 48.2 %copy-start.2 = (s32[16]{0:T(128)S(1)}, s32[16]{0:T(128)}, u32[]{:S(2)}) copy-start(s32[16]{0:T(128)} %latent_counts_ref.1) | copy-start | bytes 196
  4.5 48.2 %all-to-all-start = ((bf16[16,4,128,128]{3,2,1,0:T(8,128)(2,1)}), bf16[16,4,128,128]{3,2,1,0:T(8,128)(2,1)S(1)}, u32[]{:S(2)}, u32[]{:S(2)}) async-start(bf16[16,4,128,128]{3,2,1,0:T(8,128)(2,1)} %get-tuple-element.12), calls=%async_computation | async-start | bytes 4194304 | tf_op jit(solution)/shard_map/all_to_all | solution.py:329
  61.3 9.4 %collective-permute-start = (bf16[4,4,48,256]{3,2,1,0:T(8,128)(2,1)}, bf16[4,4,48,256]{3,2,1,0:T(8,128)(2,1)S(1)}, u32[]{:S(2)}, u32[]{:S(2)}) collective-permute-start(bf16[4,4,48,256]{3,2,1,0:T(8,128)(2,1)} %get-tuple-element.17), channel_id=1, source_target_pairs={{0,32},{32,0},{1,33},{33,1},{2,34},{34,2},{3,35},{35,3},{4,36},{36... | collective-permute-start | bytes 1179656 | tf_op jit(solution)/shard_map/ppermute | solution.py:289
  63.3 43.9 %all-to-all-start.1 = ((bf16[16,4,128,128]{3,2,1,0:T(8,128)(2,1)}), bf16[16,4,128,128]{3,2,1,0:T(8,128)(2,1)S(1)}, u32[]{:S(2)}, u32[]{:S(2)}) async-start(bf16[16,4,128,128]{3,2,1,0:T(8,128)(2,1)} %get-tuple-element.13), calls=%async_computation.1 | async-start | bytes 4194304 | tf_op jit(solution)/shard_map/all_to_all | solution.py:336
  70.9 9.2 %collective-permute-start.1 = (bf16[4,48,256]{2,1,0:T(8,128)(2,1)S(1)}, bf16[4,48,256]{2,1,0:T(8,128)(2,1)S(1)}, u32[]{:S(2)}, u32[]{:S(2)}) collective-permute-start(bf16[4,48,256]{2,1,0:T(8,128)(2,1)S(1)} %get-tuple-element.22), channel_id=1, source_target_pairs={{0,64},{64,0},{128,192},{192,128},{256,320},{320,256},{384,448},{4... | collective-permute-start | bytes 294920 | tf_op jit(solution)/shard_map/ppermute | solution.py:296
  72.8 8.3 %collective-permute-start.3 = (bf16[4,48,256]{2,1,0:T(8,128)(2,1)S(1)}, bf16[4,48,256]{2,1,0:T(8,128)(2,1)S(1)}, u32[]{:S(2)}, u32[]{:S(2)}) collective-permute-start(bf16[4,48,256]{2,1,0:T(8,128)(2,1)S(1)} %get-tuple-element.23), channel_id=1, source_target_pairs={{0,192},{64,128},{128,64},{192,0},{256,448},{320,384},{384,320},{4... | collective-permute-start | bytes 294920 | tf_op jit(solution)/shard_map/ppermute | solution.py:296
  76.4 10.3 %collective-permute-start.2 = (bf16[4,48,256]{2,1,0:T(8,128)(2,1)S(1)}, bf16[4,48,256]{2,1,0:T(8,128)(2,1)S(1)}, u32[]{:S(2)}, u32[]{:S(2)}) collective-permute-start(bf16[4,48,256]{2,1,0:T(8,128)(2,1)S(1)} %get-tuple-element.24), channel_id=1, source_target_pairs={{0,128},{64,192},{128,0},{192,64},{256,384},{320,448},{384,256},{4... | collective-permute-start | bytes 294920 | tf_op jit(solution)/shard_map/ppermute | solution.py:296
  86.8 10.1 %collective-permute-start.5 = (bf16[48,256]{1,0:T(8,128)(2,1)S(1)}, bf16[48,256]{1,0:T(8,128)(2,1)S(1)}, u32[]{:S(2)}, u32[]{:S(2)}) collective-permute-start(bf16[48,256]{1,0:T(8,128)(2,1)S(1)} %get-tuple-element.26), channel_id=1, source_target_pairs={{0,256},{64,320},{128,384},{192,448},{256,16},{320,80},{384,144},{... | collective-permute-start | bytes 73736 | tf_op jit(solution)/shard_map/ppermute | solution.py:304
  91.9 10.0 %collective-permute-start.4 = (bf16[48,256]{1,0:T(8,128)(2,1)S(1)}, bf16[48,256]{1,0:T(8,128)(2,1)S(1)}, u32[]{:S(2)}, u32[]{:S(2)}) collective-permute-start(bf16[48,256]{1,0:T(8,128)(2,1)S(1)} %get-tuple-element.25), channel_id=1, source_target_pairs={{0,272},{64,336},{128,400},{192,464},{256,0},{320,64},{384,128},{4... | collective-permute-start | bytes 73736 | tf_op jit(solution)/shard_map/ppermute | solution.py:304
  96.9 9.6 %collective-permute-start.6 = (bf16[48,256]{1,0:T(8,128)(2,1)S(1)}, bf16[48,256]{1,0:T(8,128)(2,1)S(1)}, u32[]{:S(2)}, u32[]{:S(2)}) collective-permute-start(bf16[48,256]{1,0:T(8,128)(2,1)S(1)} %fusion.4), channel_id=1, source_target_pairs={{0,256},{64,320},{128,384},{192,448},{256,16},{320,80},{384,144},{... | collective-permute-start | bytes 73736 | tf_op jit(solution)/shard_map/ppermute | solution.py:304

commit v5 on v4

--- a/solution.py
+++ b/solution.py
@@ -211,21 +211,21 @@
     def _():
         core_index = seg_index % cores
         pair_index = seg_index // cores
-        fars = pairs // NEAR
+        chips = keep_ref.shape[0] * keep_ref.shape[1]
         slot = lax.broadcasted_iota(jnp.int32, (slots, dim), 0)
-        for near in range(NEAR):
-            for block in range(fars):
-                pair = block * NEAR + ((pair_index % NEAR) ^ near)
-                shift = (pl.program_id(0) - half_index) * fars + block - pair_index // NEAR
-                shift = (shift + keep_ref.shape[1]) % keep_ref.shape[1]
-                for ref, core in ((keep_ref, core_index), (send_ref, 1 - core_index)):
-                    segment = pair * cores + core
-                    at = pl.ds(starts_ref[segment], slots)
-                    own = slot < starts_ref[segment + 1] - starts_ref[segment]
-                    key_part = jnp.where(own, key_sum_ref[at, :] * scaling, 0.0)
-                    value_part = jnp.where(own, value_sum_ref[at, :], 0.0)
-                    ref[near, shift, :, :dim] = key_part.astype(ref.dtype)
-                    ref[near, shift, :, dim:] = value_part.astype(ref.dtype)
+        for pair in range(pairs):
+            distance = (pl.program_id(0) - half_index) * pairs + pair - pair_index
+            distance = (distance + chips) % chips
+            near = distance % NEAR
+            far = (distance + 1) // NEAR % keep_ref.shape[1]
+            for ref, core in ((keep_ref, core_index), (send_ref, 1 - core_index)):
+                segment = pair * cores + core
+                at = pl.ds(starts_ref[segment], slots)
+                own = slot < starts_ref[segment + 1] - starts_ref[segment]
+                key_part = jnp.where(own, key_sum_ref[at, :] * scaling, 0.0)
+                value_part = jnp.where(own, value_sum_ref[at, :], 0.0)
+                ref[near, far, :, :dim] = key_part.astype(ref.dtype)
+                ref[near, far, :, dim:] = value_part.astype(ref.dtype)
 
 
 def attend_heads(place, text_counts, latent_counts, latents, visible_turned, text, groups):
@@ -284,29 +284,30 @@
     )(place, text_counts, latent_counts, latents, visible_turned, text)
 
 
+def shift(piece, by):
+    pairs = lax.axis_size("z_lo")
+    chips = pairs * lax.axis_size("z_hi")
+    place = [z % pairs * 2 + z // pairs for z in range(chips)]
+    steps = [(place[z], place[(z + by) % chips]) for z in range(chips)]
+    return lax.ppermute(piece.astype(jnp.bfloat16), ("z_lo", "z_hi"), steps)
+
+
+def stage(pieces, by):
+    passing = shift(pieces[2], by)
+    left = shift(pieces[3], -by)
+    right = shift(pieces[1] + passing.astype(jnp.float32), by)
+    return pieces[0], left.astype(jnp.float32), right.astype(jnp.float32)
+
+
 def add_up(keep, send):
-    pairs = lax.axis_size("z_lo")
     other = lax.ppermute(send, "core", [(0, 1), (1, 0)])
-    keep = keep.astype(jnp.float32) + other.astype(jnp.float32)
-    send = keep[1:].astype(jnp.bfloat16)
-    keep = keep[0]
-    arrived = []
-    for near in range(1, NEAR):
-        steps = [(i, i ^ near) for i in range(pairs)]
-        arrived.append(lax.ppermute(send[near - 1], "z_lo", steps))
-    for other in arrived:
-        keep = keep + other.astype(jnp.float32)
-    chips = pairs * lax.axis_size("z_hi")
-
-    def shift(piece, by):
-        flat = lambda z: z % pairs * 2 + z // pairs
-        steps = [(flat(z), flat((z + by) % chips)) for z in range(chips)]
-        return lax.ppermute(piece.astype(jnp.bfloat16), ("z_lo", "z_hi"), steps)
-
-    passing = shift(keep[2], NEAR)
-    left = shift(keep[3], -NEAR)
-    right = shift(keep[1] + passing.astype(jnp.float32), NEAR)
-    return (keep[0] + left.astype(jnp.float32) + right.astype(jnp.float32)).astype(jnp.bfloat16)
+    own, left, right = stage(keep.astype(jnp.float32) + other.astype(jnp.float32), 1)
+    own, left, right = stage(own + left + right, NEAR)
+    dim = own.shape[1] // 2
+    return tuple(
+        (own[:, at] + left[:, at] + right[:, at]).astype(jnp.bfloat16)
+        for at in (slice(0, dim), slice(dim, None))
+    )
 
 
 def shards(
@@ -321,7 +322,6 @@
 ):
     halves = lax.axis_size("z_hi")
     peers = lax.axis_size("x") * lax.axis_size("y")
-    dim = latent_keys.shape[1]
     place = lax.axis_index(("z_lo", "core", "z_hi")).astype(jnp.int32).reshape(1)
     text, packed = spread(
         gate_logits, queries, cotangent, latent_keys, latent_values, halves, peers
@@ -334,9 +334,9 @@
         place, text_counts, latent_counts, latents, visibility.T, text, groups=8
     )
     out = lax.all_to_all(out, ("x", "y"), split_axis=0, concat_axis=0, tiled=True)
-    grads = add_up(keep, send)
+    grad_keys, grad_values = add_up(keep, send)
     mixed_rows, grad_queries = collect(out)
-    return (mixed_rows, grad_queries, grads[:, :dim], grads[:, dim:])
+    return (mixed_rows, grad_queries, grad_keys, grad_values)
 
 
 def solution(mesh):

time: 110 us -> 109 us (level)
    ppermute x3 -> x0, starting transfers between devices: 9.21 us -> none  [add_up(): arrived.append(lax.ppermute(send[near - 1], 'z_lo', steps))]
    ppermute x3 -> x6, starting transfers between devices: 14.8 us -> 23.6 us  [shift(): return lax.ppermute(piece.astype(jnp.bfloat16), ('z_lo', 'z_hi'), steps)]
    ppermute x3 -> x0, waiting for transfers between devices: 6.59 us -> none  [add_up(): arrived.append(lax.ppermute(send[near - 1], 'z_lo', steps))]
    ppermute x3 -> x6, waiting for transfers between devices: 4.96 us -> 11.2 us  [shift(): return lax.ppermute(piece.astype(jnp.bfloat16), ('z_lo', 'z_hi'), steps)]
  transfers between devices with their start and end apart: 9 -> 9, of which waited for: 4 -> 3; matrix products, arithmetic and copies ran while one was open for 1% -> 1% of each run, Pallas kernels for 0% -> 0%
where the time goes in v5:
time: 109 us
  starting transfers between devices  42.6 us (39%)
  blocking collectives  38.6 us (35%)
  Pallas kernels  13.9 us (13%)
  waiting for transfers between devices  11.2 us (10%)
  between operations  1.45 us (1%)
    all_gather x1, blocking collectives, shards(): latents = lax.all_gather(packed, ('z_hi', 'z_lo'), axis=0, tiled=True)  36.2 us
    ppermute x6, starting transfers between devices, shift(): return lax.ppermute(piece.astype(jnp.bfloat16), ('z_lo', 'z_hi'), steps)  23.6 us
    ppermute x6, waiting for transfers between devices, shift(): return lax.ppermute(piece.astype(jnp.bfloat16), ('z_lo', 'z_hi'), steps)  11.2 us
    all_to_all x1, starting transfers between devices, shards(): lax.all_to_all(text, ('x', 'y'), split_axis=0, concat_axis=0, tiled=True)  9.55 us
    pallas_call x1, Pallas kernels, attend_heads(): pl.pallas_call(heads_kernel, grid_spec=grid_spec, out_shape=[pltpu.HBM(te...  8.73 us
    all_to_all x1, starting transfers between devices, shards(): lax.all_to_all(out, ('x', 'y'), split_axis=0, concat_axis=0, tiled=True)  7.39 us
    pallas_call x1, Pallas kernels, spread(): pl.pallas_call(spread_kernel, in_specs=[vmem] * 5, out_specs=[vmem, vmem]...  3.24 us
    all_gather x1, blocking collectives, shards(): latents = lax.all_gather(latents, 'core', axis=0, tiled=True)  2.45 us
  transfers between devices with their start and end apart: 9, of which 3 were waited for; matrix products, arithmetic and copies ran while one was open for 1% of the time, Pallas kernels for 0%

profile of v5, /device:TPU:6, one launch (start us, length us, event | category | flops | bytes accessed | tf_op | source)
XLA Modules:
  0.0 108.7 jit_solution(15745181953825211964)
XLA Ops:
  1.3 3.2 %spread.1 = (bf16[16,4,128,128]{3,2,1,0:T(8,128)(2,1)}, bf16[56,256]{1,0:T(8,128)(2,1)}) custom-call(f32[1,1]{1,0:T(1,128)} %bitcast.33.gate_ref, bf16[128,4096]{1,0:T(8,128)(2,1)} %query_ref.1, bf16[128,4096]{1,0:T(8,128)(2,1)} %grad_ref.1, bf16[48,128]{1,0:T(8,128)(2,1)} %latent_key_ref.1, bf16[48,128]{1,0:T(8,128)(2,1)} %latent_value_ref.1), custom_call_target="tpu_custom_call" | custom-call | bytes 4194304 | tf_op jit(solution)/shard_map/spread/pallas_call | solution.py:46
  4.5 0.0 copy-start.3
  4.5 0.0 copy-start
  4.5 0.0 copy-start.1
  4.5 0.0 copy-start.2
  4.5 9.5 %all-to-all-start = ((bf16[16,4,128,128]{3,2,1,0:T(8,128)(2,1)}), bf16[16,4,128,128]{3,2,1,0:T(8,128)(2,1)S(1)}, u32[]{:S(2)}, u32[]{:S(2)}) async-start(bf16[16,4,128,128]{3,2,1,0:T(8,128)(2,1)} %get-tuple-element.12), calls=%async_computation | async-start | bytes 4194304 | tf_op jit(solution)/shard_map/all_to_all | solution.py:329
  14.1 0.0 copy-done.3
  14.1 36.2 %all_gather.6 = bf16[896,256]{1,0:T(8,128)(2,1)S(1)} all-gather(bf16[56,256]{1,0:T(8,128)(2,1)S(1)} %copy-done.3), channel_id=1, replica_groups=mesh['z_lo'=8,'core'=2,'z_hi'=2,'x'=4,'y'=4] {'z_hi','z_lo'}, dimensions={0}, use_global_device_ids=true | all-gather | bytes 487424 | tf_op jit(solution)/shard_map/all_gather | solution.py:330
  50.3 2.5 %all_gather.7 = bf16[1792,256]{1,0:T(8,128)(2,1)S(1)} all-gather(bf16[896,256]{1,0:T(8,128)(2,1)S(1)} %all_gather.6), channel_id=1, replica_groups=mesh['z_lo'=8,'core'=2,'z_hi'=2,'x'=4,'y'=4] {'core'}, dimensions={0}, use_global_device_ids=true | all-gather | bytes 1376256 | tf_op jit(solution)/shard_map/all_gather | solution.py:331
  52.7 0.0 all-to-all-done.text_ref
  52.7 0.0 copy-done
  52.7 0.0 copy-done.1
  52.7 0.0 copy-done.2
  52.7 8.7 %attend_heads.1 = (bf16[16,4,128,128]{3,2,1,0:T(8,128)(2,1)}, bf16[4,4,48,256]{3,2,1,0:T(8,128)(2,1)S(1)}, bf16[4,4,48,256]{3,2,1,0:T(8,128)(2,1)}) custom-call(s32[1]{0:T(128)} %bitcast.place_ref, s32[16]{0:T(128)S(1)} %copy-done.1, s32[16]{0:T(128)S(1)} %copy-done.2, bf16[2,2,8,56,256]{4,3,2,1,0:T(8,128)(2,1)S(1)} %bitcast.34, s32[16,512]{1,0:T(8,128)S(1)} %bitcast.35, ...), custom_call_target="tpu_custom_call" | custom-call | flops 4831838208 | bytes 4194304 | tf_op jit(solution)/shard_map/attend_heads/pallas_call | solution.py:269
  61.5 2.0 %collective-permute-start = (bf16[4,4,48,256]{3,2,1,0:T(8,128)(2,1)}, bf16[4,4,48,256]{3,2,1,0:T(8,128)(2,1)S(1)}, u32[]{:S(2)}, u32[]{:S(2)}) collective-permute-start(bf16[4,4,48,256]{3,2,1,0:T(8,128)(2,1)} %get-tuple-element.17), channel_id=1, source_target_pairs={{0,32},{32,0},{1,33},{33,1},{2,34},{34,2},{3,35},{35,3},{4,36},{36... | collective-permute-start | bytes 1179656 | tf_op jit(solution)/shard_map/ppermute | solution.py:303
  63.5 7.4 %all-to-all-start.1 = ((bf16[16,4,128,128]{3,2,1,0:T(8,128)(2,1)}), bf16[16,4,128,128]{3,2,1,0:T(8,128)(2,1)S(1)}, u32[]{:S(2)}, u32[]{:S(2)}) async-start(bf16[16,4,128,128]{3,2,1,0:T(8,128)(2,1)} %get-tuple-element.13), calls=%async_computation.1 | async-start | bytes 4194304 | tf_op jit(solution)/shard_map/all_to_all | solution.py:336
  70.9 0.0 collective-permute-done
  70.9 0.1 fusion.8
  71.1 1.9 %collective-permute-start.2 = (bf16[4,48,256]{2,1,0:T(8,128)(2,1)S(1)}, bf16[4,48,256]{2,1,0:T(8,128)(2,1)S(1)}, u32[]{:S(2)}, u32[]{:S(2)}) collective-permute-start(bf16[4,48,256]{2,1,0:T(8,128)(2,1)S(1)} %get-tuple-element.23), channel_id=1, source_target_pairs={{0,64},{64,128},{128,192},{192,256},{256,320},{320,384},{384,448},... | collective-permute-start | bytes 294920 | tf_op jit(solution)/shard_map/ppermute | solution.py:292
  73.0 5.1 %collective-permute-start.1 = (bf16[4,48,256]{2,1,0:T(8,128)(2,1)S(1)}, bf16[4,48,256]{2,1,0:T(8,128)(2,1)S(1)}, u32[]{:S(2)}, u32[]{:S(2)}) collective-permute-start(bf16[4,48,256]{2,1,0:T(8,128)(2,1)S(1)} %get-tuple-element.22), channel_id=1, source_target_pairs={{0,464},{64,0},{128,64},{192,128},{256,192},{320,256},{384,320},{4... | collective-permute-start | bytes 294920 | tf_op jit(solution)/shard_map/ppermute | solution.py:292
  78.1 0.7 collective-permute-done.2
  78.8 1.9 %collective-permute-start.3 = (bf16[4,48,256]{2,1,0:T(8,128)(2,1)S(1)}, bf16[4,48,256]{2,1,0:T(8,128)(2,1)S(1)}, u32[]{:S(2)}, u32[]{:S(2)}) collective-permute-start(bf16[4,48,256]{2,1,0:T(8,128)(2,1)S(1)} %fusion.1), channel_id=1, source_target_pairs={{0,64},{64,128},{128,192},{192,256},{256,320},{320,384},{384,448},... | collective-permute-start | bytes 294920 | tf_op jit(solution)/shard_map/ppermute | solution.py:292
  80.7 0.0 collective-permute-done.1
  80.7 5.8 %collective-permute-done.3 = bf16[4,48,256]{2,1,0:T(8,128)(2,1)S(1)} collective-permute-done((bf16[4,48,256]{2,1,0:T(8,128)(2,1)S(1)}, bf16[4,48,256]{2,1,0:T(8,128)(2,1)S(1)}, u32[]{:S(2)}, u32[]{:S(2)}) %collective-permute-start.3) | collective-permute-done | bytes 98336 | tf_op jit(solution)/shard_map/ppermute | solution.py:292
  86.6 4.9 %collective-permute-start.5 = (bf16[48,256]{1,0:T(8,128)(2,1)S(1)}, bf16[48,256]{1,0:T(8,128)(2,1)S(1)}, u32[]{:S(2)}, u32[]{:S(2)}) collective-permute-start(bf16[48,256]{1,0:T(8,128)(2,1)S(1)} %get-tuple-element.27), channel_id=1, source_target_pairs={{0,256},{64,320},{128,384},{192,448},{256,16},{320,80},{384,144},{... | collective-permute-start | bytes 73736 | tf_op jit(solution)/shard_map/ppermute | solution.py:292
  91.5 4.9 %collective-permute-start.4 = (bf16[48,256]{1,0:T(8,128)(2,1)S(1)}, bf16[48,256]{1,0:T(8,128)(2,1)S(1)}, u32[]{:S(2)}, u32[]{:S(2)}) collective-permute-start(bf16[48,256]{1,0:T(8,128)(2,1)S(1)} %get-tuple-element.26), channel_id=1, source_target_pairs={{0,272},{64,336},{128,400},{192,464},{256,0},{320,64},{384,128},{4... | collective-permute-start | bytes 73736 | tf_op jit(solution)/shard_map/ppermute | solution.py:292
  96.3 0.0 collective-permute-done.5
  96.4 4.9 %collective-permute-start.6 = (bf16[48,256]{1,0:T(8,128)(2,1)S(1)}, bf16[48,256]{1,0:T(8,128)(2,1)S(1)}, u32[]{:S(2)}, u32[]{:S(2)}) collective-permute-start(bf16[48,256]{1,0:T(8,128)(2,1)S(1)} %fusion.5), channel_id=1, source_target_pairs={{0,256},{64,320},{128,384},{192,448},{256,16},{320,80},{384,144},{... | collective-permute-start | bytes 73736 | tf_op jit(solution)/shard_map/ppermute | solution.py:292
  101.3 0.0 collective-permute-done.4
  101.3 4.8 %collective-permute-done.6 = bf16[48,256]{1,0:T(8,128)(2,1)S(1)} collective-permute-done((bf16[48,256]{1,0:T(8,128)(2,1)S(1)}, bf16[48,256]{1,0:T(8,128)(2,1)S(1)}, u32[]{:S(2)}, u32[]{:S(2)}) %collective-permute-start.6) | collective-permute-done | bytes 24608 | tf_op jit(solution)/shard_map/ppermute | solution.py:292
  106.1 0.6 fusion.6
  106.8 0.0 all-to-all-done.1.text_ref
  106.8 1.9 %collect.1 = (bf16[128,4096]{1,0:T(8,128)(2,1)}, bf16[128,4096]{1,0:T(8,128)(2,1)}) custom-call(bf16[16,4,128,128]{3,2,1,0:T(8,128)(2,1)S(1)} %all-to-all-done.1.text_ref), custom_call_target="tpu_custom_call" | custom-call | bytes 4194304 | tf_op jit(solution)/shard_map/collect/pallas_call | solution.py:74
  (8 shorter events, 0.1 us)
Async XLA Ops:
  4.5 9.6 %copy-start.3 = (bf16[56,256]{1,0:T(8,128)(2,1)S(1)}, bf16[56,256]{1,0:T(8,128)(2,1)}, u32[]{:S(2)}) copy-start(bf16[56,256]{1,0:T(8,128)(2,1)} %get-tuple-element.11) | copy-start | bytes 86020
  4.5 48.2 %copy-start = (s32[512,16]{0,1:T(8,128)S(1)}, s32[512,16]{0,1:T(8,128)}, u32[]{:S(2)}) copy-start(s32[512,16]{0,1:T(8,128)} %param.13) | copy-start | bytes 98308
  4.5 48.2 %copy-start.1 = (s32[16]{0:T(128)S(1)}, s32[16]{0:T(128)}, u32[]{:S(2)}) copy-start(s32[16]{0:T(128)} %text_counts_ref.1) | copy-start | bytes 196
  4.5 48.2 %copy-start.2 = (s32[16]{0:T(128)S(1)}, s32[16]{0:T(128)}, u32[]{:S(2)}) copy-start(s32[16]{0:T(128)} %latent_counts_ref.1) | copy-start | bytes 196
  4.5 48.2 %all-to-all-start = ((bf16[16,4,128,128]{3,2,1,0:T(8,128)(2,1)}), bf16[16,4,128,128]{3,2,1,0:T(8,128)(2,1)S(1)}, u32[]{:S(2)}, u32[]{:S(2)}) async-start(bf16[16,4,128,128]{3,2,1,0:T(8,128)(2,1)} %get-tuple-element.12), calls=%async_computation | async-start | bytes 4194304 | tf_op jit(solution)/shard_map/all_to_all | solution.py:329
  61.5 9.4 %collective-permute-start = (bf16[4,4,48,256]{3,2,1,0:T(8,128)(2,1)}, bf16[4,4,48,256]{3,2,1,0:T(8,128)(2,1)S(1)}, u32[]{:S(2)}, u32[]{:S(2)}) collective-permute-start(bf16[4,4,48,256]{3,2,1,0:T(8,128)(2,1)} %get-tuple-element.17), channel_id=1, source_target_pairs={{0,32},{32,0},{1,33},{33,1},{2,34},{34,2},{3,35},{35,3},{4,36},{36... | collective-permute-start | bytes 1179656 | tf_op jit(solution)/shard_map/ppermute | solution.py:303
  63.5 43.3 %all-to-all-start.1 = ((bf16[16,4,128,128]{3,2,1,0:T(8,128)(2,1)}), bf16[16,4,128,128]{3,2,1,0:T(8,128)(2,1)S(1)}, u32[]{:S(2)}, u32[]{:S(2)}) async-start(bf16[16,4,128,128]{3,2,1,0:T(8,128)(2,1)} %get-tuple-element.13), calls=%async_computation.1 | async-start | bytes 4194304 | tf_op jit(solution)/shard_map/all_to_all | solution.py:336
  71.1 7.7 %collective-permute-start.2 = (bf16[4,48,256]{2,1,0:T(8,128)(2,1)S(1)}, bf16[4,48,256]{2,1,0:T(8,128)(2,1)S(1)}, u32[]{:S(2)}, u32[]{:S(2)}) collective-permute-start(bf16[4,48,256]{2,1,0:T(8,128)(2,1)S(1)} %get-tuple-element.23), channel_id=1, source_target_pairs={{0,64},{64,128},{128,192},{192,256},{256,320},{320,384},{384,448},... | collective-permute-start | bytes 294920 | tf_op jit(solution)/shard_map/ppermute | solution.py:292
  73.0 7.8 %collective-permute-start.1 = (bf16[4,48,256]{2,1,0:T(8,128)(2,1)S(1)}, bf16[4,48,256]{2,1,0:T(8,128)(2,1)S(1)}, u32[]{:S(2)}, u32[]{:S(2)}) collective-permute-start(bf16[4,48,256]{2,1,0:T(8,128)(2,1)S(1)} %get-tuple-element.22), channel_id=1, source_target_pairs={{0,464},{64,0},{128,64},{192,128},{256,192},{320,256},{384,320},{4... | collective-permute-start | bytes 294920 | tf_op jit(solution)/shard_map/ppermute | solution.py:292
  78.8 7.7 %collective-permute-start.3 = (bf16[4,48,256]{2,1,0:T(8,128)(2,1)S(1)}, bf16[4,48,256]{2,1,0:T(8,128)(2,1)S(1)}, u32[]{:S(2)}, u32[]{:S(2)}) collective-permute-start(bf16[4,48,256]{2,1,0:T(8,128)(2,1)S(1)} %fusion.1), channel_id=1, source_target_pairs={{0,64},{64,128},{128,192},{192,256},{256,320},{320,384},{384,448},... | collective-permute-start | bytes 294920 | tf_op jit(solution)/shard_map/ppermute | solution.py:292
  86.6 9.8 %collective-permute-start.5 = (bf16[48,256]{1,0:T(8,128)(2,1)S(1)}, bf16[48,256]{1,0:T(8,128)(2,1)S(1)}, u32[]{:S(2)}, u32[]{:S(2)}) collective-permute-start(bf16[48,256]{1,0:T(8,128)(2,1)S(1)} %get-tuple-element.27), channel_id=1, source_target_pairs={{0,256},{64,320},{128,384},{192,448},{256,16},{320,80},{384,144},{... | collective-permute-start | bytes 73736 | tf_op jit(solution)/shard_map/ppermute | solution.py:292
  91.5 9.8 %collective-permute-start.4 = (bf16[48,256]{1,0:T(8,128)(2,1)S(1)}, bf16[48,256]{1,0:T(8,128)(2,1)S(1)}, u32[]{:S(2)}, u32[]{:S(2)}) collective-permute-start(bf16[48,256]{1,0:T(8,128)(2,1)S(1)} %get-tuple-element.26), channel_id=1, source_target_pairs={{0,272},{64,336},{128,400},{192,464},{256,0},{320,64},{384,128},{4... | collective-permute-start | bytes 73736 | tf_op jit(solution)/shard_map/ppermute | solution.py:292
  96.4 9.8 %collective-permute-start.6 = (bf16[48,256]{1,0:T(8,128)(2,1)S(1)}, bf16[48,256]{1,0:T(8,128)(2,1)S(1)}, u32[]{:S(2)}, u32[]{:S(2)}) collective-permute-start(bf16[48,256]{1,0:T(8,128)(2,1)S(1)} %fusion.5), channel_id=1, source_target_pairs={{0,256},{64,320},{128,384},{192,448},{256,16},{320,80},{384,144},{... | collective-permute-start | bytes 73736 | tf_op jit(solution)/shard_map/ppermute | solution.py:292
